TPU v7x, 256 devices: a whole 4x4x8 slice. The times are simulated.
256 devices in a mesh: blk: 64 (over y, z, core), req: 4 (over x).
Axes of the slice: x: 4, y: 4, z: 8, core: 2. Of those that a mesh axis runs over, the one named last changes fastest.
Arguments:
- tokens_in: bfloat16 [4, 8192, 1792], P('req', 'blk'), may hold values from -6 to 6
- query_weight: bfloat16 [1792, 256], replicated, may hold values from -0.125 to 0.125
- key_weight: bfloat16 [1792, 256], replicated, may hold values from -0.125 to 0.125
- value_weight: bfloat16 [1792, 1792], replicated, may hold values from -0.125 to 0.125
- conv_weight: float32 [3, 1792], replicated, may hold values from -3 to 3
- prompt_lengths: int32 [4], P('req'), may hold values from 4096 to 8192, as said below
- decode_map: int32 [4], P('req'), may hold values from 0 to 3, each once
Outputs:
- mixed: bfloat16 [4, 8192, 1792], P('req', 'blk')
- decode_state: float32 [4, 273, 1792], P('req', None, 'blk')
- decode_norm: float32 [4, 273, 16], P('req')
Inputs may be any that keep to these rules, and one draw needn't show every extreme that they name: `prompt_lengths`: some prompt has exactly 8192 live tokens. `decode_map`: each decode slot receives exactly one prompt.
All inputs are finite; a program needn't handle non-finite values.
Results may differ from a plain program's by a relative error of at most 0.0057.
Values may be sent and summed in bfloat16 or wider, within the bound.
A program may use at most 384 MiB of HBM per device.

v0:
```python
import math

import jax
import jax.numpy as jnp
from jax import lax
from jax.sharding import PartitionSpec as P

HEADS = 16
FEAT = 16
CONV = 3


def from_behind(array, axis, by):
    devices = lax.axis_size(axis)
    pairs = [(i, i + by) for i in range(devices) if 0 <= i + by < devices]
    return lax.ppermute(array, axis, pairs)


def entering(part, axis, combine, identity):
    place = lax.axis_index(axis)
    gathered = jax.tree.map(lambda a: lax.all_gather(a, axis), part)
    state = jax.tree.map(lambda a, e: jnp.zeros_like(a) + jnp.asarray(e, a.dtype), part, identity)

    def one(turn, state):
        return combine(
            state, jax.tree.map(lambda a: lax.dynamic_index_in_dim(a, turn, 0, False), gathered)
        )

    return lax.fori_loop(0, place, one, state)


def features_last(x):
    half = x * FEAT ** (-0.25)
    outer = half[:, :, None, :] * half[:, None, :, :]
    flat = outer.reshape(half.shape[0], FEAT * FEAT, half.shape[2]) * math.sqrt(0.5)
    ones = jnp.ones((half.shape[0], 1, half.shape[2]), jnp.float32)
    return jnp.concatenate([ones, half, flat], 1)


def add_pair(earlier, later):
    return (earlier[0] + later[0], earlier[1] + later[1])


def route_slot(pair, decode_map):
    groups = lax.axis_size("req")
    slots = (jnp.arange(groups, dtype=jnp.int32) == decode_map[0]).astype(jnp.float32)
    sent = (slots[:, None, None] * pair[0][None], slots[:, None, None] * pair[1][None])
    got = (
        lax.all_to_all(sent[0], "req", split_axis=0, concat_axis=0, tiled=True),
        lax.all_to_all(sent[1], "req", split_axis=0, concat_axis=0, tiled=True),
    )
    return (jnp.sum(got[0], 0), jnp.sum(got[1], 0))


def reduce_blocks(pair):
    return (
        lax.psum_scatter(pair[0], "blk", scatter_dimension=1, tiled=True),
        lax.psum_scatter(pair[1], "blk", scatter_dimension=1, tiled=True),
    )


def on_device(
    tokens_in, query_weight, key_weight, value_weight, conv_weight, prompt_lengths, decode_map
):
    rows = tokens_in.shape[1]
    width = tokens_in.shape[2]
    blocks = lax.axis_size("blk")
    head_size = width // HEADS
    hi = lax.Precision.HIGHEST
    inputs = tokens_in[0]
    queries = jnp.einsum(
        "dk,td->kt", query_weight, inputs, preferred_element_type=jnp.float32
    ).reshape(HEADS, FEAT, rows)
    keys = jnp.einsum("dk,td->kt", key_weight, inputs, preferred_element_type=jnp.float32).reshape(
        HEADS, FEAT, rows
    )
    values = jnp.dot(inputs, value_weight, preferred_element_type=jnp.float32).astype(jnp.bfloat16)
    earlier = from_behind(values[rows - (CONV - 1) :], "blk", 1)
    extended = jnp.concatenate([earlier, values], 0).astype(jnp.float32)
    conv = jnp.zeros((rows, width), jnp.float32)
    for tap in range(CONV):
        conv = conv + conv_weight[tap][None, :] * extended[CONV - 1 - tap : CONV - 1 - tap + rows]
    conv_t = conv.astype(jnp.bfloat16).astype(jnp.float32).T.reshape(HEADS, head_size, rows)
    start = lax.axis_index("blk") * rows
    live = (start + jnp.arange(rows, dtype=jnp.int32) < prompt_lengths[0]).astype(jnp.float32)
    feat_q = features_last(queries)
    feat_k = features_last(keys) * live[None, None, :]
    own_state = jnp.einsum("hft,hct->hfc", feat_k, conv_t, precision=hi)
    own_norm = jnp.sum(feat_k, 2)
    zero_state = jnp.zeros_like(own_state)
    zero_norm = jnp.zeros_like(own_norm)
    prior_state, prior_norm = entering(
        (own_state, own_norm), "blk", add_pair, (zero_state, zero_norm)
    )
    causal = (jnp.arange(rows)[:, None] >= jnp.arange(rows)[None, :]).astype(jnp.float32)
    scores = jnp.einsum("hft,hfs->hts", feat_q, feat_k, precision=hi) * causal[None]
    num = jnp.einsum("hts,hcs->hct", scores, conv_t, precision=hi) + jnp.einsum(
        "hft,hfc->hct", feat_q, prior_state, precision=hi
    )
    den = (
        jnp.sum(scores, -1)
        + jnp.einsum("hft,hf->ht", feat_q, prior_norm, precision=hi)
        + (1.0 - live)[None, :]
    )
    result = jnp.where(live[None, None, :] > 0, num / den[:, None, :], 0.0)
    mixed = result.reshape(width, rows).T.reshape(1, rows, width).astype(jnp.bfloat16)
    state_flat = jnp.transpose(own_state, (1, 0, 2)).reshape(own_state.shape[1], width)
    pair = (state_flat, jnp.tile(own_norm.T, (1, blocks)))
    final = route_slot(reduce_blocks(pair), decode_map)
    return (mixed, final[0][None], final[1][None])


def solution(mesh):
    return jax.shard_map(
        on_device,
        mesh=mesh,
        in_specs=(P("req", "blk", None), P(), P(), P(), P(), P("req"), P("req")),
        out_specs=(P("req", "blk", None), P("req", None, "blk"), P("req", None, None)),
        check_vma=False,
    )
```

profile of v0, /device:TPU:249, one launch (start us, length us, event | category | flops | bytes accessed | tf_op | source)
XLA Modules:
  0.0 1169.6 jit_solution(267389214199181395)
XLA Ops:
  8.2 3.8 convolution_convert_fusion
  17.4 3.8 fusion.22
  23.1 3.3 reshape.79
  26.5 2.6 fusion.21
  31.4 1.8 copy.28
  38.4 6.5 fusion.23
  44.9 169.8 %all-reduce.3.cloned.1.call-done = f32[273,1792]{1,0:T(8,128)} async-done(((f32[273,1792]{1,0:T(8,128)}), f32[273,1792]{1,0:T(8,128)}) %all-reduce.3.cloned.1.call-update) | async-done | bytes 1956880
  216.6 4.0 all-to-all-start
  220.6 130.7 %reduce-scatter.3.cloned.1.call-done = f32[273,16]{0,1:T(8,128)} async-done(((f32[273,1024]{0,1:T(8,128)}), f32[273,16]{0,1:T(8,128)}) %reduce-scatter.3.cloned.1.call-update) | async-done | bytes 17488 | tf_op jit(solution)/shard_map/reduce_scatter | solution.py:58
  352.7 4.0 all-to-all-start.1
  357.3 4.0 all-to-all-done.1
  361.9 73.3 %all-gather.7.cloned.1.call-done = f32[1024,273]{1,0:T(8,128)} async-done(((f32[16,273]{1,0:T(8,128)}), f32[1024,273]{1,0:T(8,128)}) %all-gather.7.cloned.1.call-update) | async-done | bytes 1118224 | tf_op jit(solution)/shard_map/all_gather | solution.py:21
  435.2 488.8 %all-gather.5.cloned.1.call-done = f32[1024,273,112]{2,0,1:T(8,128)} async-done(((f32[16,273,112]{2,0,1:T(8,128)}), f32[1024,273,112]{2,0,1:T(8,128)}) %all-gather.5.cloned.1.call-update) | async-done | bytes 125239312 | tf_op jit(solution)/shard_map/all_gather | solution.py:21
  924.2 228.4 %while.12 = (s32[]{:T(128)}, f32[16,273,112]{2,1,0:T(8,128)S(1)}, f32[16,273]{1,0:T(8,128)S(1)}, s32[]{:T(128)}, f32[64,16,273,112]{3,1,0,2:T(8,128)}, /*index=5...) while((s32[]{:T(128)}, f32[16,273,112]{2,1,0:T(8,128)S(1)}, f32[16,273]{1,0:T(8,128)S(1)}, s32[]{:T(128)}, ...), condition=%wide.region_2.3_spmd, body=%wide.region_1.2_spmd.sunk | while | flops 493589 | bytes 9836879 | solution.py:29
  925.0 1.8 constant_dynamic-slice_fusion.3
  928.6 1.8 constant_dynamic-slice_fusion.3
  932.2 1.8 constant_dynamic-slice_fusion.3
  935.8 1.8 constant_dynamic-slice_fusion.3
  939.5 1.8 constant_dynamic-slice_fusion.3
  961.2 1.8 constant_dynamic-slice_fusion.3
  964.8 1.8 constant_dynamic-slice_fusion.3
  968.4 1.8 constant_dynamic-slice_fusion.3
  972.1 1.8 constant_dynamic-slice_fusion.3
  975.7 1.8 constant_dynamic-slice_fusion.3
  979.3 1.8 constant_dynamic-slice_fusion.3
  982.9 1.8 constant_dynamic-slice_fusion.3
  986.5 1.8 constant_dynamic-slice_fusion.3
  990.2 1.8 constant_dynamic-slice_fusion.3
  993.8 1.8 constant_dynamic-slice_fusion.3
  997.4 1.8 constant_dynamic-slice_fusion.3
  1001.0 1.8 constant_dynamic-slice_fusion.3
  1004.6 1.8 constant_dynamic-slice_fusion.3
  1008.3 1.8 constant_dynamic-slice_fusion.3
  1030.0 1.8 constant_dynamic-slice_fusion.3
  1033.6 1.8 constant_dynamic-slice_fusion.3
  1037.2 1.8 constant_dynamic-slice_fusion.3
  1040.9 1.8 constant_dynamic-slice_fusion.3
  1044.5 1.8 constant_dynamic-slice_fusion.3
  1048.1 1.8 constant_dynamic-slice_fusion.3
  1051.7 1.8 constant_dynamic-slice_fusion.3
  1055.4 1.8 constant_dynamic-slice_fusion.3
  1059.0 1.8 constant_dynamic-slice_fusion.3
  1062.6 1.8 constant_dynamic-slice_fusion.3
  1066.2 1.8 constant_dynamic-slice_fusion.3
  1069.8 1.8 constant_dynamic-slice_fusion.3
  1073.5 1.8 constant_dynamic-slice_fusion.3
  1152.6 3.5 fusion.4
  1156.2 5.2 fusion.5
  (231 shorter events, 188.6 us)
Async XLA Ops:
  7.2 1.0 copy-start
  7.2 6.8 copy-start.13
  7.2 6.9 copy-start.10
  7.2 207.5 %all-reduce.3.cloned.1.call-start = ((), (), s32[]{:S(2)}) async-start(), calls=%async_computation.6 | async-start | bytes 4014080
  12.1 4.7 collective-permute-start
  15.1 11.4 copy-start.4
  17.4 3.9 copy-start.8
  26.4 324.8 %reduce-scatter.3.cloned.1.call-start = ((), (), s32[]{:S(2)}) async-start(), calls=%async_computation.3 | async-start | bytes 1597440 | tf_op jit(solution)/shard_map/reduce_scatter | solution.py:58
  29.1 1.4 copy-start.12
  30.4 404.8 %all-gather.7.cloned.1.call-start = ((), (), s32[]{:S(2)}) async-start(), calls=%async_computation.5 | async-start | bytes 1597440 | tf_op jit(solution)/shard_map/all_gather | solution.py:21
  31.1 892.9 %all-gather.5.cloned.1.call-start = ((), (), s32[]{:S(2)}) async-start(), calls=%async_computation.4 | async-start | bytes 145367040 | tf_op jit(solution)/shard_map/all_gather | solution.py:21
  33.2 1.2 copy-start.11
  33.2 1.8 copy-start.14
  35.0 3.4 copy-start.1
  36.3 2.1 copy-start.5
  36.7 0.7 copy-start.6
  37.0 1.4 copy-start.2
  216.6 136.1 %all-to-all-start = ((f32[4,273,28]{1,2,0:T(8,128)}), f32[4,273,28]{1,2,0:T(8,128)S(1)}, u32[]{:S(2)}, u32[]{:S(2)}) async-start(f32[4,273,28]{1,2,0:T(8,128)} %broadcast_multiply_fusion), calls=%async_computation | async-start | bytes 393216 | tf_op jit(solution)/shard_map/all_to_all | solution.py:49
  352.7 8.6 all-to-all-start.1
  924.2 228.4 %copy-start.7 = (f32[16,16,128]{2,1,0:T(8,128)S(1)}, f32[16,16,128]{2,1,0:T(8,128)}, u32[]{:S(2)}) copy-start(f32[16,16,128]{2,1,0:T(8,128)} %copy-done.6) | copy-start | bytes 393220
  1152.6 3.6 copy-start.3
  1156.2 5.2 copy-start.9
  1156.2 5.2 copy-start.15
Sparse Core Ops, SparseCore 0:
  26.5 188.0 all-reduce.2
  218.7 132.4 reduce-scatter.2
  354.4 80.7 all-gather.6
  437.9 486.0 all-gather.4
where the time goes:
time: 1180 us; the launch traced here: 1170 us
  waiting for transfers between devices  867 us (73%)
  local copies, waits for them, and re-layouts  130 us (11%)
  other arithmetic  120 us (10%)
  matrix products  24.4 us (2%)
  between operations  16.2 us (1%)
    all_gather x2, waiting for transfers between devices, entering(): gathered = jax.tree.map(lambda a: lax.all_gather(a, axis), part)  562 us
    unnamed x5, waiting for transfers between devices  170 us
    reduce_scatter x1, waiting for transfers between devices, reduce_blocks(): lax.psum_scatter(pair[1], 'blk', scatter_dimension=1, tiled=True)  131 us
    dynamic_slice x63, local copies, waits for them, and re-layouts, one(): lax.dynamic_index_in_dim(a, turn, 0, False)  114 us
    add x126, other arithmetic, add_pair(): return (earlier[0] + later[0], earlier[1] + later[1])  113 us
  transfers between devices with their start and end apart: 7, of which 5 were waited for; matrix products, arithmetic and copies ran while one was open for 2% of the time, Pallas kernels for 0%

commit v1 on v0

v1 whole, which is shorter than its diff:
```python
import math

import jax
import jax.numpy as jnp
import numpy as np
from jax import lax
from jax.experimental import pallas as pl
from jax.experimental.pallas import tpu as pltpu
from jax.sharding import PartitionSpec as P

HEADS = 16
FEAT = 16
CONV = 3
D = 1792
HV = 112
EXPAND = 273
XS, YS, ZS = 4, 4, 8
HALF = HEADS // 2
COLS = HALF * HV
TOK = 128
CHIP = 2 * TOK
HALO = 16
ROWS = 160
LANES = 128
MESH = pl.DeviceIdType.MESH
VCHUNKS = ((0, 256), (256, 256), (512, 256), (768, 128))
F32 = jnp.float32
BF16 = jnp.bfloat16


def selection():
    sel = np.zeros((280, ROWS), np.float32)
    sel[0, 152] = 1.0
    for a in range(16):
        sel[1 + a, a] = 1.0
        for b in range(16):
            row = 17 + 16 * a + b
            r = (b - a) % 16
            if r == 0:
                sel[row, 16 + a] = 1.0
            elif r < 8:
                sel[row, 16 + 16 * r + a] = math.sqrt(0.5)
            elif r > 8:
                sel[row, 16 + 16 * (16 - r) + b] = math.sqrt(0.5)
            else:
                sel[row, 144 + min(a, b)] = math.sqrt(0.5)
    return sel


def pickers():
    pick = np.zeros((HALF, HALF, LANES), np.float32)
    for i in range(HALF):
        pick[i, i, HV + 1] = 1.0
        pick[i, i, HV + 2] = 1.0
    return pick


def features(heads_t, yy, extra):
    yy[:, 0:16, :] = heads_t
    yy[:, 16:32, :] = heads_t
    parts = [heads_t, heads_t * heads_t * math.sqrt(0.5)]
    for r in range(1, 8):
        parts.append(heads_t * yy[:, r : r + 16, :])
    parts.append(heads_t[:, 0:8] * heads_t[:, 8:16])
    row = lax.broadcasted_iota(jnp.int32, (HALF, 8, CHIP), 1)
    parts.append(jnp.where(row == 0, 1.0, 0.0).astype(F32))
    phi = jnp.concatenate(parts, 1)
    if extra is not None:
        phi = phi * extra
    return phi


def kernel(
    tok, wq, wk, wv, cw, plen, dmap, sel, pick,
    mixed, dstate, dnorm,
    xs, wqk_v, wv_v, cw_v, sel_v, pick_v,
    vbuf, cvb, vp, yy, phik, phiq, ktb, numb, gsend, gat, tsend, ty, psend, pbuf,
    dt, dsend, dbuf, nsend, nbuf, obuf,
    lsem, xsend, xrecv, gs, gr, ys, yr, ps, pr, dsm, dr, ns, nr, osm, orm,
):
    x = lax.axis_index("req")
    blk = lax.axis_index("blk")
    c = blk % 2
    chip = blk // 2
    z = chip % ZS
    y = chip // ZS
    mine = (z % 2) * 4 + z // 2

    def dev(x_, y_, z_, c_):
        return ((y_ * ZS + z_) * 2 + c_, x_)

    nxt = (chip + 1) % (YS * ZS)
    prv = (chip + YS * ZS - 1) % (YS * ZS)

    def remote(src, dst, send, recv, device):
        return pltpu.make_async_remote_copy(
            src_ref=src, dst_ref=dst, send_sem=send, recv_sem=recv, device_id=device, device_id_type=MESH
        )

    half = pl.multiple_of(COLS * c, 128)
    khalf = pl.multiple_of(128 * c, 128)
    own_rows = pl.multiple_of(HALO + TOK * c, 16)
    loads = [
        pltpu.make_async_copy(wk.at[:, pl.ds(khalf, 128)], wqk_v.at[:, 0:128], lsem.at[0]),
        pltpu.make_async_copy(wq.at[:, pl.ds(khalf, 128)], wqk_v.at[:, 128:256], lsem.at[1]),
        pltpu.make_async_copy(tok, xs.at[pl.ds(own_rows, TOK)], lsem.at[2]),
        pltpu.make_async_copy(cw.at[:, pl.ds(half, COLS)], cw_v, lsem.at[3]),
    ]
    for n, (at, size) in enumerate(VCHUNKS):
        loads.append(
            pltpu.make_async_copy(
                wv.at[:, pl.ds(pl.multiple_of(half + at, 128), size)], wv_v.at[:, at : at + size], lsem.at[4 + n]
            )
        )
    loads.append(pltpu.make_async_copy(sel, sel_v, lsem.at[8]))
    loads.append(pltpu.make_async_copy(pick, pick_v, lsem.at[9]))
    for copy in loads:
        copy.start()

    pair = z - z % 2
    barrier = pltpu.get_barrier_semaphore()
    partners = []
    for cc in range(2):
        partners.append((nxt * 2 + cc, x))
        partners.append((prv * 2 + cc, x))
    for d in range(1, ZS):
        partners.append(dev(x, y, (z + d) % ZS, c))
    for d in range(1, YS):
        partners.append(dev(x, (y + d) % YS, z, c))
    me4 = (z % 2) * 2 + c
    for dx in range(XS):
        for dm in range(4):
            if dx == 0 and dm == 0:
                continue
            member = (me4 + dm) % 4
            partners.append(dev((x + dx) % XS, y, pair + member // 2, member % 2))
    for device in partners:
        pl.semaphore_signal(barrier, inc=1, device_id=device, device_id_type=MESH)
    pl.semaphore_wait(barrier, len(partners))

    to_sib = remote(tok, xs.at[pl.ds(own_rows, TOK)], xsend.at[0], xrecv.at[0], dev(x, y, z, 1 - c))
    to_sib.start()
    tail = tok.at[TOK - HALO : TOK]
    halo0 = remote(tail, xs.at[0:HALO], xsend.at[1], xrecv.at[1], (nxt * 2, x))
    halo1 = remote(tail, xs.at[0:HALO], xsend.at[2], xrecv.at[1], (nxt * 2 + 1, x))

    @pl.when(c == 1)
    def _():
        halo0.start()
        halo1.start()

    slot = dmap[0].astype(F32)
    length = plen[0]
    lane_tok = lax.broadcasted_iota(jnp.int32, (1, CHIP), 1) + chip * CHIP
    live_row = jnp.where(lane_tok < length, 1.0, 0.0).astype(F32)
    sub_tok = lax.broadcasted_iota(jnp.int32, (CHIP, 1), 0) + chip * CHIP
    live_col = jnp.where(sub_tok < length, 1.0, 0.0).astype(F32)
    lane = lax.broadcasted_iota(jnp.int32, (1, LANES), 1)

    loads[0].wait()
    loads[1].wait()
    loads[2].wait()
    other_rows = pl.multiple_of(HALO + TOK * (1 - c), 16)
    remote(tok, xs.at[pl.ds(other_rows, TOK)], xsend.at[0], xrecv.at[0], dev(x, y, z, 1 - c)).wait_recv()
    remote(tail, xs.at[0:HALO], xsend.at[1], xrecv.at[1], (prv * 2 + 1, x)).wait_recv()

    qk = jnp.dot(xs[HALO:, :], wqk_v[...], preferred_element_type=F32)
    keys_t = qk[:, 0:128].T
    ktb[...] = keys_t.astype(BF16)
    phi = features(keys_t.reshape(HALF, FEAT, CHIP) * 0.5, yy, live_row[None])
    phik[...] = phi.astype(BF16)

    loads[3].wait()
    first = (chip > 0).astype(F32)
    for n, (at, size) in enumerate(VCHUNKS):
        loads[4 + n].wait()
        val = jnp.dot(xs[...], wv_v[:, at : at + size], preferred_element_type=F32)
        vbuf[:, at : at + size] = val.astype(BF16).astype(F32)
        vbuf[0:HALO, at : at + size] = vbuf[0:HALO, at : at + size] * first
        conv = jnp.zeros((CHIP, size), F32)
        for tap in range(CONV):
            conv = conv + cw_v[tap : tap + 1, at : at + size] * vbuf[HALO - tap : HALO - tap + CHIP, at : at + size]
        cvb[:, at : at + size] = conv
    for i in range(HALF):
        tile, off = (HV * i) // 128, (HV * i) % 128
        width = 128 if off + HV <= 128 else 256
        wide = cvb[:, 128 * tile : 128 * tile + width]
        if off:
            wide = pltpu.roll(wide, width - off, 1)
        head = jnp.where(lane < HV, wide[:, 0:128], jnp.where(lane == HV, 1.0, 0.0))
        vp[i] = head.astype(BF16)

    sends = []
    for d in range(1, ZS):
        zt = (z + d) % ZS
        i = (zt % 2) * 4 + zt // 2
        gsend[i] = jnp.dot(phik[i], vp[i], preferred_element_type=F32).astype(BF16)
        copy = remote(gsend.at[i], gat.at[z], gs.at[d], gr.at[z], dev(x, y, zt, c))
        copy.start()
        sends.append(copy)
    gat[z] = jnp.dot(phik[mine], vp[mine], preferred_element_type=F32).astype(BF16)

    queries = qk[:, 128:256]
    phi_q = features((queries.T).reshape(HALF, FEAT, CHIP) * 0.5, yy, None)
    for i in range(HALF):
        phiq[i] = phi_q[i].T.astype(BF16)
    row_t = lax.broadcasted_iota(jnp.int32, (CHIP, CHIP), 0)
    col_s = lax.broadcasted_iota(jnp.int32, (CHIP, CHIP), 1)
    causal = jnp.where(row_t >= col_s, 1.0, 0.0).astype(F32) * live_row
    for i in range(HALF):
        one_head = jnp.where(lane // FEAT == i, queries, 0.0).astype(BF16)
        dots = jnp.dot(one_head, ktb[...], preferred_element_type=F32) * 0.25
        weights = (1.0 + dots + 0.5 * dots * dots) * causal
        numb[i] = jnp.dot(weights.astype(BF16), vp[i], preferred_element_type=F32)

    for d in range(1, ZS):
        zf = (z + ZS - d) % ZS
        remote(gat.at[zf], gat.at[zf], gs.at[0], gr.at[zf], dev(x, y, zf, c)).wait_recv()
    total = gat[0].astype(F32)
    for zz in range(1, ZS):
        total = total + gat[zz].astype(F32)
    tsend[...] = total.astype(BF16)
    for d in range(1, YS):
        copy = remote(tsend, ty.at[y], ys.at[d], yr.at[y], dev(x, (y + d) % YS, z, c))
        copy.start()
        sends.append(copy)
    ty[y] = total.astype(BF16)
    for d in range(1, YS):
        yf = (y + YS - d) % YS
        remote(tsend, ty.at[yf], ys.at[0], yr.at[yf], dev(x, yf, z, c)).wait_recv()
    before = jnp.zeros((ROWS, LANES), F32)
    whole = jnp.zeros((ROWS, LANES), F32)
    for yy_ in range(YS):
        piece = ty[yy_].astype(F32)
        whole = whole + piece
        before = before + piece * (yy_ < y).astype(F32)
    norm_next = pltpu.roll(whole, 1, 1)
    norm_hi = norm_next.astype(BF16).astype(F32)
    norm_lo = pltpu.roll(norm_next - norm_hi, 1, 1)
    for zz in range(ZS):
        tile = jnp.where(lane == HV + 1, norm_hi, jnp.where(lane == HV + 2, norm_lo, before))
        psend[zz] = tile.astype(BF16)
        before = before + gat[zz].astype(F32)
    for d in range(1, ZS):
        zt = (z + d) % ZS
        copy = remote(psend.at[zt], pbuf.at[mine], ps.at[d], pr.at[mine], dev(x, y, zt, c))
        copy.start()
        sends.append(copy)
    pbuf[mine] = psend[z]

    sender = (z % 2 == y % 2) & (c == y // 2)
    flagged = jnp.concatenate([whole, jnp.zeros((256 - ROWS, LANES), F32) + slot], 0)
    dt[...] = flagged.T
    for sub in range(4):
        dsend[sub] = dt[28 * sub : 28 * sub + 32, :]
    dcopies = []
    for dx in range(XS):
        for dm in range(4):
            if dx == 0 and dm == 0:
                continue
            member = (me4 + dm) % 4
            dcopies.append(
                remote(
                    dsend.at[member], dbuf.at[x], dsm.at[dx * 4 + dm], dr.at[x],
                    dev((x + dx) % XS, y, pair + member // 2, member % 2),
                )
            )

    @pl.when(sender)
    def _():
        for copy in dcopies:
            copy.start()
        dbuf[x] = dsend[me4]

    for d in range(1, ZS):
        zf = (z + ZS - d) % ZS
        i = (zf % 2) * 4 + zf // 2
        remote(pbuf.at[i], pbuf.at[i], ps.at[0], pr.at[i], dev(x, y, zf, c)).wait_recv()
    loads[8].wait()
    loads[9].wait()
    norm_t = jnp.zeros((HALF, ROWS), F32)
    for i in range(HALF):
        norm_t = norm_t + lax.dot_general(
            pick_v[i], pbuf[i], (((1,), (1,)), ((), ())), preferred_element_type=F32
        )
    nsend[0] = norm_t
    nsend[1] = jnp.zeros((HALF, ROWS), F32) + slot
    nbuf[x * 2 + c, 0] = norm_t
    nbuf[x * 2 + c, 1] = jnp.zeros((HALF, ROWS), F32) + slot
    for dx in range(XS):
        for dc in range(2):
            if dx == 0 and dc == 0:
                continue
            k = dx * 2 + dc
            copy = remote(
                nsend, nbuf.at[x * 2 + c], ns.at[k], nr.at[x * 2 + c],
                dev((x + dx) % XS, y, z, (c + dc) % 2),
            )
            copy.start()
            sends.append(copy)

    for i in range(HALF):
        num = numb[i] + jnp.dot(phiq[i], pbuf[i], preferred_element_type=F32)
        den = num[:, HV : HV + 1] + (1.0 - live_col)
        numb[i] = jnp.where(live_col > 0, num / den, 0.0)
    for j in range(7):
        left = numb[j]
        if j:
            left = pltpu.roll(left, 128 - 16 * j, 1)
        right = pltpu.roll(numb[j + 1], HV - 16 * j, 1)
        obuf[:, 128 * j : 128 * j + 128] = jnp.where(lane < HV - 16 * j, left, right).astype(BF16)
    theirs = pl.multiple_of(TOK * (1 - c), 128)
    ours = pl.multiple_of(TOK * c, 128)
    other_half = pl.multiple_of(COLS * (1 - c), 128)
    out_send = remote(
        obuf.at[pl.ds(theirs, TOK)], mixed.at[:, pl.ds(half, COLS)], osm.at[0], orm.at[0], dev(x, y, z, 1 - c)
    )
    out_send.start()
    out_own = pltpu.make_async_copy(obuf.at[pl.ds(ours, TOK)], mixed.at[:, pl.ds(half, COLS)], lsem.at[10])
    out_own.start()

    here = x.astype(F32)
    for xf in range(XS):

        @pl.when(jnp.logical_not(sender & (x == xf)))
        def _():
            remote(dsend.at[0], dbuf.at[xf], dsm.at[0], dr.at[xf], dev(x, y, z, 1 - c)).wait_recv()

    state_t = jnp.zeros((32, ROWS), F32)
    for xf in range(XS):
        got = dbuf[xf]
        state_t = state_t + jnp.where(got[:, 255:256] == here, got[:, 0:ROWS], 0.0)
    full = lax.dot_general(
        sel_v[...], state_t, (((1,), (1,)), ((), ())), precision=lax.Precision.HIGHEST, preferred_element_type=F32
    )
    dstate[...] = full[0:EXPAND, 0:28]

    for dx in range(XS):
        for dc in range(2):
            if dx == 0 and dc == 0:
                continue
            src = ((x + dx) % XS) * 2 + (c + dc) % 2
            remote(nsend, nbuf.at[src], ns.at[0], nr.at[src], dev((x + dx) % XS, y, z, (c + dc) % 2)).wait_recv()
    halves = []
    for cc in range(2):
        norm = jnp.zeros((HALF, ROWS), F32)
        for xf in range(XS):
            norm = norm + jnp.where(nbuf[xf * 2 + cc, 1] == here, nbuf[xf * 2 + cc, 0], 0.0)
        halves.append(norm)
    norms = jnp.concatenate(halves, 0)
    full = lax.dot_general(
        sel_v[...], norms, (((1,), (1,)), ((), ())), precision=lax.Precision.HIGHEST, preferred_element_type=F32
    )
    dnorm[...] = full[0:EXPAND, :]

    out_own.wait()
    out_send.wait_send()
    remote(
        obuf.at[pl.ds(theirs, TOK)], mixed.at[:, pl.ds(other_half, COLS)], osm.at[0], orm.at[0], dev(x, y, z, 1 - c)
    ).wait_recv()
    to_sib.wait_send()

    @pl.when(c == 1)
    def _():
        halo0.wait_send()
        halo1.wait_send()

    for copy in sends:
        copy.wait_send()

    @pl.when(sender)
    def _():
        for copy in dcopies:
            copy.wait_send()


def on_device(tokens_in, query_weight, key_weight, value_weight, conv_weight, prompt_lengths, decode_map):
    sel = jnp.asarray(selection())
    pick = jnp.asarray(pickers(), BF16)
    any_space = pl.BlockSpec(memory_space=pl.ANY)
    vmem = pl.BlockSpec(memory_space=pltpu.VMEM)
    smem = pl.BlockSpec(memory_space=pltpu.SMEM)
    dma = pltpu.SemaphoreType.DMA
    mixed, dstate, dnorm = pl.pallas_call(
        kernel,
        out_shape=(
            jax.ShapeDtypeStruct((TOK, D), BF16),
            jax.ShapeDtypeStruct((EXPAND, 28), F32),
            jax.ShapeDtypeStruct((EXPAND, HEADS), F32),
        ),
        in_specs=[any_space] * 5 + [smem] * 2 + [any_space] * 2,
        out_specs=(any_space, vmem, vmem),
        scratch_shapes=[
            pltpu.VMEM((HALO + CHIP, D), BF16),
            pltpu.VMEM((D, 256), BF16),
            pltpu.VMEM((D, COLS), BF16),
            pltpu.VMEM((CONV, COLS), F32),
            pltpu.VMEM((280, ROWS), F32),
            pltpu.VMEM((HALF, HALF, LANES), BF16),
            pltpu.VMEM((HALO + CHIP, COLS), F32),
            pltpu.VMEM((CHIP, COLS), F32),
            pltpu.VMEM((HALF, CHIP, LANES), BF16),
            pltpu.VMEM((HALF, 32, CHIP), F32),
            pltpu.VMEM((HALF, ROWS, CHIP), BF16),
            pltpu.VMEM((HALF, CHIP, ROWS), BF16),
            pltpu.VMEM((LANES, CHIP), BF16),
            pltpu.VMEM((HALF, CHIP, LANES), F32),
            pltpu.VMEM((HALF, ROWS, LANES), BF16),
            pltpu.VMEM((ZS, ROWS, LANES), BF16),
            pltpu.VMEM((ROWS, LANES), BF16),
            pltpu.VMEM((YS, ROWS, LANES), BF16),
            pltpu.VMEM((ZS, ROWS, LANES), BF16),
            pltpu.VMEM((HALF, ROWS, LANES), BF16),
            pltpu.VMEM((LANES, 256), F32),
            pltpu.VMEM((4, 32, 256), F32),
            pltpu.VMEM((XS, 32, 256), F32),
            pltpu.VMEM((2, HALF, ROWS), F32),
            pltpu.VMEM((2 * XS, 2, HALF, ROWS), F32),
            pltpu.VMEM((CHIP, COLS), BF16),
            dma((11,)),
            dma((3,)),
            dma((2,)),
            dma((8,)),
            dma((8,)),
            dma((4,)),
            dma((4,)),
            dma((8,)),
            dma((8,)),
            dma((16,)),
            dma((4,)),
            dma((8,)),
            dma((8,)),
            dma((1,)),
            dma((1,)),
        ],
        compiler_params=pltpu.CompilerParams(
            collective_id=0, has_side_effects=True, vmem_limit_bytes=48 * 1024 * 1024
        ),
        cost_estimate=pl.CostEstimate(flops=2_000_000_000, bytes_accessed=8_000_000, transcendentals=0),
        name="taylor_attention",
    )(
        tokens_in[0], query_weight, key_weight, value_weight, conv_weight, prompt_lengths, decode_map, sel, pick
    )
    return (mixed[None], dstate[None], dnorm[None])


def solution(mesh):
    return jax.shard_map(
        on_device,
        mesh=mesh,
        in_specs=(P("req", "blk", None), P(), P(), P(), P(), P("req"), P("req")),
        out_specs=(P("req", "blk", None), P("req", None, "blk"), P("req", None, None)),
        check_vma=False,
    )
```

time: 1180 us -> 58.8 us (0.05)
  the two profiles are of different devices: /device:TPU:249 before, /device:TPU:1 now
where the time goes in v1:
time: 58.8 us; the launch traced here: 58.2 us
  Pallas kernels  48.3 us (82%)
  local copies, waits for them, and re-layouts  8 us (14%)
  between operations  1.95 us (3%)
    pallas_call x1, Pallas kernels, on_device(): pl.pallas_call(kernel, out_shape=(jax.ShapeDtypeStruct((TOK, D), BF16), j...  48.3 us
    unnamed x15, local copies, waits for them, and re-layouts  8 us

profile of v1, /device:TPU:1, one launch (start us, length us, event | category | flops | bytes accessed | tf_op | source)
XLA Modules:
  0.0 58.2 jit_solution(5365827990752091750)
XLA Ops:
  1.9 0.0 copy-start
  1.9 1.2 %copy-done = bf16[1792,256]{1,0:T(8,128)(2,1)S(1)} copy-done((bf16[1792,256]{1,0:T(8,128)(2,1)S(1)}, bf16[1792,256]{1,0:T(8,128)(2,1)}, u32[]{:S(2)}) %copy-start) | copy-done | bytes 917528
  3.1 0.0 copy-start.1
  3.1 1.2 %copy-done.1 = bf16[1792,256]{1,0:T(8,128)(2,1)S(1)} copy-done((bf16[1792,256]{1,0:T(8,128)(2,1)S(1)}, bf16[1792,256]{1,0:T(8,128)(2,1)}, u32[]{:S(2)}) %copy-start.1) | copy-done | bytes 917528
  4.3 0.0 copy-start.2
  4.3 1.0 %copy-done.2 = bf16[1,128,1792]{2,1,0:T(8,128)(2,1)S(1)} copy-done((bf16[1,128,1792]{2,1,0:T(8,128)(2,1)S(1)}, bf16[1,128,1792]{2,1,0:T(8,128)(2,1)}, u32[]{:S(2)}) %copy-start.2) | copy-done | bytes 458776
  5.3 0.0 copy-start.3
  5.3 1.0 %copy-done.3 = f32[280,160]{1,0:T(8,128)S(1)} copy-done((f32[280,160]{1,0:T(8,128)S(1)}, f32[280,160]{1,0:T(8,128)}, u32[]{:S(2)}) %copy-start.3) | copy-done | bytes 179224
  6.3 0.0 copy-start.4
  6.3 0.7 %copy-done.4 = f32[3,1792]{1,0:T(4,128)S(1)} copy-done((f32[3,1792]{1,0:T(4,128)S(1)}, f32[3,1792]{1,0:T(4,128)}, u32[]{:S(2)}) %copy-start.4) | copy-done | bytes 21528
  7.0 0.0 copy-start.5
  7.0 0.7 %copy-done.5 = bf16[8,8,128]{2,1,0:T(8,128)(2,1)S(1)} copy-done((bf16[8,8,128]{2,1,0:T(8,128)(2,1)S(1)}, bf16[8,8,128]{2,1,0:T(8,128)(2,1)}, u32[]{:S(2)}) %copy-start.5) | copy-done | bytes 16408
  7.7 48.3 %taylor_attention.1 = (bf16[128,1792]{1,0:T(8,128)(2,1)S(1)}, f32[273,28]{1,0:T(8,128)S(1)}, f32[273,16]{1,0:T(8,128)S(1)}) custom-call(bf16[128,1792]{1,0:T(8,128)(2,1)S(1)} %bitcast.5, bf16[1792,256]{1,0:T(8,128)(2,1)S(1)} %copy-done, bf16[1792,256]{1,0:T(8,128)(2,1)S(1)} %copy-done.1, bf16[1792,1792]{1,0:T(8,128)(2,1)} %wv.1, f32[3,1792]{1,0:T(4,128)S(1)} %copy-done.4, ...), custom_call_target="tpu_custom_call" | custom-call | flops 2000000000 | bytes 8000000 | tf_op jit(solution)/shard_map/taylor_attention/pallas_call | solution.py:384
  56.0 0.7 %copy.12 = f32[1,273,28]{1,0,2:T(1,128)} copy(f32[1,273,28]{2,1,0:T(8,128)S(1)} %bitcast.7) | data formatting | bytes 61152
  56.8 0.7 %copy.13 = f32[1,273,16]{1,2,0:T(8,128)} copy(f32[1,273,16]{2,1,0:T(8,128)S(1)} %bitcast.6) | data formatting | bytes 34944
  57.5 0.8 %copy.17 = bf16[1,128,1792]{2,1,0:T(8,128)(2,1)} copy(bf16[1,128,1792]{2,1,0:T(8,128)(2,1)S(1)} %bitcast.4) | data formatting | bytes 917504
Async XLA Ops:
  1.9 1.2 %copy-start = (bf16[1792,256]{1,0:T(8,128)(2,1)S(1)}, bf16[1792,256]{1,0:T(8,128)(2,1)}, u32[]{:S(2)}) copy-start(bf16[1792,256]{1,0:T(8,128)(2,1)} %wq.1) | copy-start | bytes 2752516
  3.1 1.2 %copy-start.1 = (bf16[1792,256]{1,0:T(8,128)(2,1)S(1)}, bf16[1792,256]{1,0:T(8,128)(2,1)}, u32[]{:S(2)}) copy-start(bf16[1792,256]{1,0:T(8,128)(2,1)} %wk.1) | copy-start | bytes 2752516
  4.3 1.0 %copy-start.2 = (bf16[1,128,1792]{2,1,0:T(8,128)(2,1)S(1)}, bf16[1,128,1792]{2,1,0:T(8,128)(2,1)}, u32[]{:S(2)}) copy-start(bf16[1,128,1792]{2,1,0:T(8,128)(2,1)} %param.9) | copy-start | bytes 1376260
  5.3 1.0 %copy-start.3 = (f32[280,160]{1,0:T(8,128)S(1)}, f32[280,160]{1,0:T(8,128)}, u32[]{:S(2)}) copy-start(f32[280,160]{1,0:T(8,128)} %constant.4.clone.sel) | copy-start | bytes 537604
  6.3 0.7 %copy-start.4 = (f32[3,1792]{1,0:T(4,128)S(1)}, f32[3,1792]{1,0:T(4,128)}, u32[]{:S(2)}) copy-start(f32[3,1792]{1,0:T(4,128)} %cw.1) | copy-start | bytes 64516
  7.0 0.7 %copy-start.5 = (bf16[8,8,128]{2,1,0:T(8,128)(2,1)S(1)}, bf16[8,8,128]{2,1,0:T(8,128)(2,1)}, u32[]{:S(2)}) copy-start(bf16[8,8,128]{2,1,0:T(8,128)(2,1)} %constant.5.clone.pick) | copy-start | bytes 49156

commit v2 on v1

v2 whole, which is shorter than its diff:
```python
import math

import jax
import jax.numpy as jnp
import numpy as np
from jax import lax
from jax.experimental import pallas as pl
from jax.experimental.pallas import tpu as pltpu
from jax.sharding import PartitionSpec as P

HEADS = 16
FEAT = 16
CONV = 3
D = 1792
HV = 112
EXPAND = 273
XS, YS, ZS = 4, 4, 8
HALF = HEADS // 2
COLS = HALF * HV
TOK = 128
CHIP = 2 * TOK
HALO = 16
ROWS = 160
LANES = 128
MESH = pl.DeviceIdType.MESH
VCHUNKS = ((0, 256), (256, 256), (512, 256), (768, 128))
FAR_FIRST = (4, 3, 5, 2, 6, 1, 7)
PARTS = 2
PART = ROWS // PARTS
F32 = jnp.float32
BF16 = jnp.bfloat16


def selection():
    sel = np.zeros((384, ROWS), np.float32)
    sel[0, 152] = 1.0
    for a in range(16):
        sel[1 + a, a] = 1.0
        for b in range(16):
            row = 17 + 16 * a + b
            r = (b - a) % 16
            if r == 0:
                sel[row, 16 + a] = 1.0
            elif r < 8:
                sel[row, 16 + 16 * r + a] = math.sqrt(0.5)
            elif r > 8:
                sel[row, 16 + 16 * (16 - r) + b] = math.sqrt(0.5)
            else:
                sel[row, 144 + min(a, b)] = math.sqrt(0.5)
    return sel.T.copy()


def features(heads_t, yy, extra):
    yy[:, 0:16, :] = heads_t
    yy[:, 16:32, :] = heads_t
    parts = [heads_t, heads_t * heads_t * math.sqrt(0.5)]
    for r in range(1, 8):
        parts.append(heads_t * yy[:, r : r + 16, :])
    parts.append(heads_t[:, 0:8] * heads_t[:, 8:16])
    row = lax.broadcasted_iota(jnp.int32, (HALF, 8, CHIP), 1)
    parts.append(jnp.where(row == 0, 1.0, 0.0).astype(F32))
    phi = jnp.concatenate(parts, 1)
    if extra is not None:
        phi = phi * extra
    return phi


def kernel(
    tok, wq, wk, wv, cw, plen, dmap, sel,
    mixed, dstate, dnorm,
    xs, wqk_v, wv_v, cw_v, sel_v,
    qkb, vbuf, cvb, vp, yy, phik, phiq, ktb, numb, gsend, gat, tsend, ty, psend, pbuf,
    wholeb, dt, dsend, dbuf, drt, dfin, nsend, nxb, nzs, nzb, nss, nfull, obuf,
    lsem, xsend, xrecv, gs, gr, ys, yr, ps, pr, dsm, dr, des, der, ns, nr, nzsm, nzr, nps, npr, osm, orm,
):
    x = lax.axis_index("req")
    blk = lax.axis_index("blk")
    c = blk % 2
    chip = blk // 2
    z = chip % ZS
    y = chip // ZS

    def head_of(z_):
        return (z_ % 2) * 4 + z_ // 2

    mine = head_of(z)

    def dev(x_, y_, z_, c_):
        return ((y_ * ZS + z_) * 2 + c_, x_)

    nxt = (chip + 1) % (YS * ZS)
    prv = (chip + YS * ZS - 1) % (YS * ZS)
    sibling = dev(x, y, z, 1 - c)
    pair = z - z % 2
    lead = dev(x, y, pair + y % 2, y // 2)
    leads = (z % 2 == y % 2) & (c == y // 2)
    leads_int = leads.astype(jnp.int32)
    me4 = (z % 2) * 2 + c

    def remote(src, dst, send, recv, device):
        return pltpu.make_async_remote_copy(
            src_ref=src, dst_ref=dst, send_sem=send, recv_sem=recv, device_id=device, device_id_type=MESH
        )

    half = pl.multiple_of(COLS * c, 128)
    khalf = pl.multiple_of(128 * c, 128)
    loads = [
        pltpu.make_async_copy(tok, xs.at[0:TOK], lsem.at[0]),
        pltpu.make_async_copy(wk.at[:, pl.ds(khalf, 128)], wqk_v.at[:, 0:128], lsem.at[1]),
        pltpu.make_async_copy(wq.at[:, pl.ds(khalf, 128)], wqk_v.at[:, 128:256], lsem.at[2]),
        pltpu.make_async_copy(cw.at[:, pl.ds(half, COLS)], cw_v, lsem.at[3]),
    ]
    for n, (at, size) in enumerate(VCHUNKS):
        loads.append(
            pltpu.make_async_copy(
                wv.at[:, pl.ds(pl.multiple_of(half + at, 128), size)], wv_v.at[:, at : at + size], lsem.at[4 + n]
            )
        )
    loads.append(pltpu.make_async_copy(sel, sel_v, lsem.at[8]))
    for copy in loads:
        copy.start()

    barrier = pltpu.get_barrier_semaphore()

    def here_i_am(device):
        pl.semaphore_signal(barrier, inc=1, device_id=device, device_id_type=MESH)

    here_i_am(sibling)
    here_i_am((prv * 2 + 1, x))
    for d in FAR_FIRST:
        here_i_am(dev(x, y, (z + d) % ZS, c))
    for d in range(1, YS):
        here_i_am(dev(x, (y + d) % YS, z, c))
    for d in range(1, XS):
        here_i_am(dev((x + d) % XS, y, z, c))

    @pl.when(jnp.logical_not(leads))
    def _():
        here_i_am(lead)

    pl.semaphore_wait(barrier, 1 + (ZS - 1) + (YS - 1) + (XS - 1) + 2 * c + 3 * leads_int)

    to_sib = remote(tok, xs.at[TOK:CHIP], xsend.at[0], xrecv.at[0], sibling)
    to_sib.start()
    tail = tok.at[TOK - HALO : TOK]
    halo0 = remote(tail, xs.at[CHIP : CHIP + HALO], xsend.at[1], xrecv.at[1], (nxt * 2, x))
    halo1 = remote(tail, xs.at[CHIP : CHIP + HALO], xsend.at[2], xrecv.at[1], (nxt * 2 + 1, x))

    @pl.when(c == 1)
    def _():
        halo0.start()
        halo1.start()

    slot = dmap[0].astype(F32)
    length = plen[0]
    lane_tok = lax.broadcasted_iota(jnp.int32, (1, CHIP), 1) + chip * CHIP
    live_row = jnp.where(lane_tok < length, 1.0, 0.0).astype(F32)
    sub_tok = lax.broadcasted_iota(jnp.int32, (CHIP, 1), 0) + chip * CHIP
    live_col = jnp.where(sub_tok < length, 1.0, 0.0).astype(F32)
    lane = lax.broadcasted_iota(jnp.int32, (1, LANES), 1)

    ours = pl.multiple_of(TOK * c, TOK)
    theirs = pl.multiple_of(TOK * (1 - c), TOK)
    v_ours = pl.multiple_of(HALO + TOK * c, HALO)
    v_theirs = pl.multiple_of(HALO + TOK * (1 - c), HALO)
    for n in range(3):
        loads[n].wait()
    qkb[pl.ds(ours, TOK), :] = jnp.dot(xs[0:TOK, :], wqk_v[...], preferred_element_type=F32)
    for n, (at, size) in enumerate(VCHUNKS):
        loads[4 + n].wait()
        val = jnp.dot(xs[0:TOK, :], wv_v[:, at : at + size], preferred_element_type=F32)
        vbuf[pl.ds(v_ours, TOK), at : at + size] = val.astype(BF16).astype(F32)
    to_sib.wait_recv()
    qkb[pl.ds(theirs, TOK), :] = jnp.dot(xs[TOK:CHIP, :], wqk_v[...], preferred_element_type=F32)
    halo1.wait_recv()

    keys_t = qkb[:, 0:128].T
    ktb[...] = keys_t.astype(BF16)
    phi = features(keys_t.reshape(HALF, FEAT, CHIP) * 0.5, yy, live_row[None])
    phik[...] = phi.astype(BF16)

    loads[3].wait()
    first = (chip > 0).astype(F32)
    for n, (at, size) in enumerate(VCHUNKS):
        val = jnp.dot(xs[TOK:, :], wv_v[:, at : at + size], preferred_element_type=F32)
        val = val.astype(BF16).astype(F32)
        vbuf[pl.ds(v_theirs, TOK), at : at + size] = val[0:TOK]
        vbuf[0:HALO, at : at + size] = val[TOK:] * first
    for n, (at, size) in enumerate(VCHUNKS):
        conv = jnp.zeros((CHIP, size), F32)
        for tap in range(CONV):
            conv = conv + cw_v[tap : tap + 1, at : at + size] * vbuf[HALO - tap : HALO - tap + CHIP, at : at + size]
        cvb[:, at : at + size] = conv
    for i in range(HALF):
        tile, off = (HV * i) // 128, (HV * i) % 128
        width = 128 if off + HV <= 128 else 256
        wide = cvb[:, 128 * tile : 128 * tile + width]
        if off:
            wide = pltpu.roll(wide, width - off, 1)
        head = jnp.where(lane < HV, wide[:, 0:128], jnp.where(lane == HV, 1.0, 0.0))
        vp[i] = head.astype(BF16)

    sends = [to_sib]
    for n in range(PARTS):
        part = slice(n * PART, (n + 1) * PART)
        for d in FAR_FIRST:
            zt = (z + d) % ZS
            i = head_of(zt)
            gsend[i, part] = jnp.dot(phik[i, part], vp[i], preferred_element_type=F32).astype(BF16)
            copy = remote(gsend.at[i, part], gat.at[z, part], gs.at[n, d], gr.at[n, z], dev(x, y, zt, c))
            copy.start()
            sends.append(copy)
        gat[z, part] = jnp.dot(phik[mine, part], vp[mine], preferred_element_type=F32).astype(BF16)

    queries = qkb[:, 128:256]
    phi_q = features((queries.T).reshape(HALF, FEAT, CHIP) * 0.5, yy, None)
    for i in range(HALF):
        phiq[i] = phi_q[i].T.astype(BF16)
    row_t = lax.broadcasted_iota(jnp.int32, (CHIP, CHIP), 0)
    col_s = lax.broadcasted_iota(jnp.int32, (CHIP, CHIP), 1)
    causal = jnp.where(row_t >= col_s, 1.0, 0.0).astype(F32) * live_row
    for i in range(HALF):
        one_head = jnp.where(lane // FEAT == i, queries, 0.0).astype(BF16)
        dots = jnp.dot(one_head, ktb[...], preferred_element_type=F32) * 0.25
        weights = (1.0 + dots + 0.5 * dots * dots) * causal
        numb[i] = jnp.dot(weights.astype(BF16), vp[i], preferred_element_type=F32)

    for n in range(PARTS):
        part = slice(n * PART, (n + 1) * PART)
        for d in FAR_FIRST:
            zf = (z + ZS - d) % ZS
            remote(gat.at[zf, part], gat.at[zf, part], gs.at[n, d], gr.at[n, zf], sibling).wait_recv()
        total = gat[0, part].astype(F32)
        for zz in range(1, ZS):
            total = total + gat[zz, part].astype(F32)
        tsend[part] = total.astype(BF16)
        for d in (2, 1, 3):
            copy = remote(
                tsend.at[part], ty.at[y, part], ys.at[n, d], yr.at[n, y], dev(x, (y + d) % YS, z, c)
            )
            copy.start()
            sends.append(copy)
        ty[y, part] = total.astype(BF16)

    for n in range(PARTS):
        part = slice(n * PART, (n + 1) * PART)
        for d in (2, 1, 3):
            yf = (y + YS - d) % YS
            remote(tsend.at[part], ty.at[yf, part], ys.at[n, d], yr.at[n, yf], sibling).wait_recv()
        before = jnp.zeros((PART, LANES), F32)
        whole = jnp.zeros((PART, LANES), F32)
        for yf in range(YS):
            piece = ty[yf, part].astype(F32)
            whole = whole + piece
            before = before + piece * (yf < y).astype(F32)
        wholeb[part] = whole
        for zz in range(ZS):
            psend[zz, part] = before.astype(BF16)
            before = before + gat[zz, part].astype(F32)
        for d in FAR_FIRST:
            zt = (z + d) % ZS
            copy = remote(psend.at[zt, part], pbuf.at[mine, part], ps.at[n, d], pr.at[n, mine], dev(x, y, zt, c))
            copy.start()
            sends.append(copy)
        pbuf[mine, part] = psend[z, part]

    here = x.astype(F32)
    wholeb[ROWS:] = jnp.zeros((256 - ROWS, LANES), F32) + slot
    dt[...] = wholeb[...].T
    for sub in range(4):
        dsend[sub] = dt[28 * sub : 28 * sub + 32, :]
    nsend[...] = dt[HV : HV + 8, :]
    nxb[x] = nsend[...]
    d_copies, e_copies = [], []
    for d in range(1, XS):
        copy = remote(nsend, nxb.at[x], ns.at[d], nr.at[x], dev((x + d) % XS, y, z, c))
        copy.start()
        sends.append(copy)
        d_copies.append(remote(dsend, dbuf.at[x], dsm.at[d], dr.at[x], dev((x + d) % XS, y, z, c)))

    @pl.when(leads)
    def _():
        for copy in d_copies:
            copy.start()
        dbuf[x] = dsend[...]

    for d in range(1, XS):
        xf = (x + d) % XS
        remote(nsend, nxb.at[xf], ns.at[d], nr.at[xf], sibling).wait_recv()
    routed = jnp.zeros((8, 256), F32)
    for xf in range(XS):
        routed = routed + jnp.where(nxb[xf, :, 255:256] == here, nxb[xf], 0.0)
    nzs[...] = routed
    nzb[mine] = routed
    for d in FAR_FIRST:
        copy = remote(nzs, nzb.at[mine], nzsm.at[d], nzr.at[mine], dev(x, y, (z + d) % ZS, c))
        copy.start()
        sends.append(copy)

    for d in range(1, 4):
        member = (me4 + d) % 4
        e_copies.append(
            remote(drt.at[member], dfin, des.at[d], der.at[0], dev(x, y, pair + member // 2, member % 2))
        )

    @pl.when(leads)
    def _():
        for d in range(1, XS):
            xf = (x + d) % XS
            remote(dsend, dbuf.at[xf], dsm.at[d], dr.at[xf], sibling).wait_recv()
        state = jnp.zeros((4, 32, 256), F32)
        for xf in range(XS):
            state = state + jnp.where(dbuf[xf, :, :, 255:256] == here, dbuf[xf], 0.0)
        drt[...] = state
        for copy in e_copies:
            copy.start()
        dfin[...] = drt[me4]

    def finish(i):
        num = numb[i] + jnp.dot(phiq[i], pbuf[i], preferred_element_type=F32)
        den = num[:, HV : HV + 1] + (1.0 - live_col)
        numb[i] = num * (live_col / den)

    finish(mine)
    for d in FAR_FIRST:
        zf = (z + ZS - d) % ZS
        i = head_of(zf)
        for n in range(PARTS):
            part = slice(n * PART, (n + 1) * PART)
            remote(pbuf.at[i, part], pbuf.at[i, part], ps.at[n, d], pr.at[n, i], sibling).wait_recv()
        finish(i)

    for d in FAR_FIRST:
        i = head_of((z + ZS - d) % ZS)
        remote(nzs, nzb.at[i], nzsm.at[d], nzr.at[i], sibling).wait_recv()
    nss[...] = jnp.concatenate([nzb[i, 0:1, :] for i in range(HALF)], 0)
    nfull[c] = nss[...]
    to_sib_n = remote(nss, nfull.at[c], nps.at[0], npr.at[0], sibling)
    to_sib_n.start()
    sends.append(to_sib_n)

    for j in range(7):
        left = numb[j]
        if j:
            left = pltpu.roll(left, 128 - 16 * j, 1)
        right = pltpu.roll(numb[j + 1], HV - 16 * j, 1)
        obuf[:, 128 * j : 128 * j + 128] = jnp.where(lane < HV - 16 * j, left, right).astype(BF16)
    other_half = pl.multiple_of(COLS * (1 - c), 128)
    out_send = remote(obuf.at[pl.ds(theirs, TOK)], mixed.at[:, pl.ds(half, COLS)], osm.at[0], orm.at[0], sibling)
    out_send.start()
    sends.append(out_send)
    out_own = pltpu.make_async_copy(obuf.at[pl.ds(ours, TOK)], mixed.at[:, pl.ds(half, COLS)], lsem.at[9])
    out_own.start()

    loads[8].wait()

    @pl.when(jnp.logical_not(leads))
    def _():
        remote(dfin, dfin, des.at[0], der.at[0], sibling).wait_recv()

    full = jnp.dot(dfin[:, 0:ROWS], sel_v[...], precision=lax.Precision.HIGHEST, preferred_element_type=F32)
    dstate[...] = full[0:28, None, 0:EXPAND]
    to_sib_n.wait_recv()
    norms = nfull[...].reshape(HEADS, 256)[:, 0:ROWS]
    full = jnp.dot(norms, sel_v[...], precision=lax.Precision.HIGHEST, preferred_element_type=F32)
    dnorm[...] = full[:, 0:EXPAND]

    out_own.wait()
    remote(
        obuf.at[pl.ds(theirs, TOK)], mixed.at[:, pl.ds(other_half, COLS)], osm.at[0], orm.at[0], sibling
    ).wait_recv()
    for copy in sends:
        copy.wait_send()

    @pl.when(c == 1)
    def _():
        halo0.wait_send()
        halo1.wait_send()

    @pl.when(leads)
    def _():
        for copy in d_copies + e_copies:
            copy.wait_send()


def on_device(tokens_in, query_weight, key_weight, value_weight, conv_weight, prompt_lengths, decode_map):
    sel = jnp.asarray(selection())
    hbm = pl.BlockSpec(memory_space=pltpu.HBM)
    any_space = pl.BlockSpec(memory_space=pl.ANY)
    vmem = pl.BlockSpec(memory_space=pltpu.VMEM)
    smem = pl.BlockSpec(memory_space=pltpu.SMEM)
    dma = pltpu.SemaphoreType.DMA
    mixed, dstate, dnorm = pl.pallas_call(
        kernel,
        out_shape=(
            jax.ShapeDtypeStruct((TOK, D), BF16),
            jax.ShapeDtypeStruct((28, 1, EXPAND), F32),
            jax.ShapeDtypeStruct((HEADS, EXPAND), F32),
        ),
        in_specs=[hbm] * 5 + [smem] * 2 + [hbm],
        out_specs=(any_space, vmem, vmem),
        scratch_shapes=[
            pltpu.VMEM((CHIP + HALO, D), BF16),
            pltpu.VMEM((D, 256), BF16),
            pltpu.VMEM((D, COLS), BF16),
            pltpu.VMEM((CONV, COLS), F32),
            pltpu.VMEM((ROWS, 384), F32),
            pltpu.VMEM((CHIP, 256), F32),
            pltpu.VMEM((HALO + CHIP, COLS), F32),
            pltpu.VMEM((CHIP, COLS), F32),
            pltpu.VMEM((HALF, CHIP, LANES), BF16),
            pltpu.VMEM((HALF, 32, CHIP), F32),
            pltpu.VMEM((HALF, ROWS, CHIP), BF16),
            pltpu.VMEM((HALF, CHIP, ROWS), BF16),
            pltpu.VMEM((LANES, CHIP), BF16),
            pltpu.VMEM((HALF, CHIP, LANES), F32),
            pltpu.VMEM((HALF, ROWS, LANES), BF16),
            pltpu.VMEM((ZS, ROWS, LANES), BF16),
            pltpu.VMEM((ROWS, LANES), BF16),
            pltpu.VMEM((YS, ROWS, LANES), BF16),
            pltpu.VMEM((ZS, ROWS, LANES), BF16),
            pltpu.VMEM((HALF, ROWS, LANES), BF16),
            pltpu.VMEM((256, LANES), F32),
            pltpu.VMEM((LANES, 256), F32),
            pltpu.VMEM((4, 32, 256), F32),
            pltpu.VMEM((XS, 4, 32, 256), F32),
            pltpu.VMEM((4, 32, 256), F32),
            pltpu.VMEM((32, 256), F32),
            pltpu.VMEM((8, 256), F32),
            pltpu.VMEM((XS, 8, 256), F32),
            pltpu.VMEM((8, 256), F32),
            pltpu.VMEM((HALF, 8, 256), F32),
            pltpu.VMEM((HALF, 256), F32),
            pltpu.VMEM((2, HALF, 256), F32),
            pltpu.VMEM((CHIP, COLS), BF16),
            dma((10,)),
            dma((3,)),
            dma((2,)),
            dma((PARTS, ZS)),
            dma((PARTS, ZS)),
            dma((PARTS, YS)),
            dma((PARTS, YS)),
            dma((PARTS, ZS)),
            dma((PARTS, ZS)),
            dma((XS,)),
            dma((XS,)),
            dma((4,)),
            dma((1,)),
            dma((XS,)),
            dma((XS,)),
            dma((ZS,)),
            dma((ZS,)),
            dma((1,)),
            dma((1,)),
            dma((1,)),
            dma((1,)),
        ],
        compiler_params=pltpu.CompilerParams(
            collective_id=0, has_side_effects=True, vmem_limit_bytes=40 * 1024 * 1024
        ),
        cost_estimate=pl.CostEstimate(flops=2_000_000_000, bytes_accessed=8_000_000, transcendentals=0),
        name="taylor_attention",
    )(*[pltpu.with_memory_space_constraint(a, pltpu.HBM) for a in (tokens_in[0], query_weight, key_weight, value_weight, conv_weight)], prompt_lengths, decode_map, pltpu.with_memory_space_constraint(sel, pltpu.HBM))
    return (mixed[None], jnp.transpose(dstate, (1, 2, 0)), jnp.transpose(dnorm)[None])


def solution(mesh):
    return jax.shard_map(
        on_device,
        mesh=mesh,
        in_specs=(P("req", "blk", None), P(), P(), P(), P(), P("req"), P("req")),
        out_specs=(P("req", "blk", None), P("req", None, "blk"), P("req", None, None)),
        check_vma=False,
    )
```

time: 58.8 us -> 44.2 us (0.75)
  Pallas kernels: 48.3 us -> 40.2 us
  local copies, waits for them, and re-layouts: 8 us -> 1.99 us
    pallas_call x1, Pallas kernels: 48.3 us -> 40.2 us  [on_device(): pl.pallas_call(kernel, out_shape=(jax.ShapeDtypeStruct((TOK, D), BF16), j...]
    unnamed x15 -> x3, local copies, waits for them, and re-layouts: 8 us -> 1.99 us
where the time goes in v2:
time: 44.2 us; the launch traced here: 44.1 us
  Pallas kernels  40.2 us (91%)
  local copies, waits for them, and re-layouts  1.99 us (5%)
  between operations  1.93 us (4%)
    pallas_call x1, Pallas kernels, on_device(): pl.pallas_call(kernel, out_shape=(jax.ShapeDtypeStruct((TOK, D), BF16), j...  40.2 us
    unnamed x3, local copies, waits for them, and re-layouts  1.99 us

profile of v2, /device:TPU:1, one launch (start us, length us, event | category | flops | bytes accessed | tf_op | source)
XLA Modules:
  0.0 44.1 jit_solution(9850157026791937614)
XLA Ops:
  1.9 40.2 %taylor_attention.1 = (bf16[128,1792]{1,0:T(8,128)(2,1)S(1)}, f32[28,1,273]{2,1,0:T(1,128)S(1)}, f32[16,273]{1,0:T(8,128)S(1)}) custom-call(bf16[128,1792]{1,0:T(8,128)(2,1)} %bitcast.9, bf16[1792,256]{1,0:T(8,128)(2,1)} %wq.1, bf16[1792,256]{1,0:T(8,128)(2,1)} %wk.1, bf16[1792,1792]{1,0:T(8,128)(2,1)} %wv.1, f32[3,1792]{1,0:T(4,128)} %cw.1, ...), custom_call_target="tpu_custom_call" | custom-call | flops 2000000000 | bytes 8000000 | tf_op jit(solution)/shard_map/taylor_attention/pallas_call | solution.py:393
  42.1 0.8 %copy.16 = bf16[1,128,1792]{2,1,0:T(8,128)(2,1)} copy(bf16[1,128,1792]{2,1,0:T(8,128)(2,1)S(1)} %bitcast.6) | data formatting | bytes 917504
  42.9 0.6 %copy.17 = f32[1,273,28]{1,0,2:T(1,128)} copy(f32[1,273,28]{1,0,2:T(1,128)S(1)} %bitcast.7) | data formatting | bytes 61152
  43.5 0.6 %copy.18 = f32[1,273,16]{1,2,0:T(8,128)} copy(f32[1,273,16]{1,2,0:T(8,128)S(1)} %bitcast.8) | data formatting | bytes 34944

commit v3 on v2

--- a/solution.py
+++ b/solution.py
@@ -70,7 +70,7 @@
     mixed, dstate, dnorm,
     xs, wqk_v, wv_v, cw_v, sel_v,
     qkb, vbuf, cvb, vp, yy, phik, phiq, ktb, numb, gsend, gat, tsend, ty, psend, pbuf,
-    wholeb, dt, dsend, dbuf, drt, dfin, nsend, nxb, nzs, nzb, nss, nfull, obuf,
+    wholeb, dt, dbuf, drt, dfin, nsend, nxb, nzs, nzb, nss, nfull, osend, orecv,
     lsem, xsend, xrecv, gs, gr, ys, yr, ps, pr, dsm, dr, des, der, ns, nr, nzsm, nzr, nps, npr, osm, orm,
 ):
     x = lax.axis_index("req")
@@ -215,7 +215,8 @@
     queries = qkb[:, 128:256]
     phi_q = features((queries.T).reshape(HALF, FEAT, CHIP) * 0.5, yy, None)
     for i in range(HALF):
-        phiq[i] = phi_q[i].T.astype(BF16)
+        for n in range(PARTS):
+            phiq[n, i] = phi_q[i, n * PART : (n + 1) * PART].T.astype(BF16)
     row_t = lax.broadcasted_iota(jnp.int32, (CHIP, CHIP), 0)
     col_s = lax.broadcasted_iota(jnp.int32, (CHIP, CHIP), 1)
     causal = jnp.where(row_t >= col_s, 1.0, 0.0).astype(F32) * live_row
@@ -253,7 +254,7 @@
             piece = ty[yf, part].astype(F32)
             whole = whole + piece
             before = before + piece * (yf < y).astype(F32)
-        wholeb[part] = whole
+        wholeb[part] = jnp.where(lane == LANES - 1, slot, whole)
         for zz in range(ZS):
             psend[zz, part] = before.astype(BF16)
             before = before + gat[zz, part].astype(F32)
@@ -265,37 +266,46 @@
         pbuf[mine, part] = psend[z, part]
 
     here = x.astype(F32)
-    wholeb[ROWS:] = jnp.zeros((256 - ROWS, LANES), F32) + slot
-    dt[...] = wholeb[...].T
-    for sub in range(4):
-        dsend[sub] = dt[28 * sub : 28 * sub + 32, :]
-    nsend[...] = dt[HV : HV + 8, :]
+    d_copies, e_copies = [], []
+    for d in (2, 1, 3):
+        d_copies.append(remote(wholeb, dbuf.at[x], dsm.at[d], dr.at[x], dev((x + d) % XS, y, z, c)))
+
+    @pl.when(leads)
+    def _():
+        for copy in d_copies:
+            copy.start()
+        dbuf[x] = wholeb[...]
+
+    row8 = lax.broadcasted_iota(jnp.int32, (8, LANES), 0)
+    pick = jnp.where((lane == HV) & (row8 == 0) | (lane == LANES - 1) & (row8 == 1), 1.0, 0.0)
+    nsend[...] = lax.dot_general(
+        pick, wholeb[...], (((1,), (1,)), ((), ())), precision=lax.Precision.HIGHEST, preferred_element_type=F32
+    )
     nxb[x] = nsend[...]
-    d_copies, e_copies = [], []
-    for d in range(1, XS):
+    for d in (2, 1, 3):
         copy = remote(nsend, nxb.at[x], ns.at[d], nr.at[x], dev((x + d) % XS, y, z, c))
         copy.start()
         sends.append(copy)
-        d_copies.append(remote(dsend, dbuf.at[x], dsm.at[d], dr.at[x], dev((x + d) % XS, y, z, c)))
-
-    @pl.when(leads)
-    def _():
-        for copy in d_copies:
-            copy.start()
-        dbuf[x] = dsend[...]
-
     for d in range(1, XS):
         xf = (x + d) % XS
         remote(nsend, nxb.at[xf], ns.at[d], nr.at[xf], sibling).wait_recv()
-    routed = jnp.zeros((8, 256), F32)
+    routed = jnp.zeros((1, ROWS), F32)
     for xf in range(XS):
-        routed = routed + jnp.where(nxb[xf, :, 255:256] == here, nxb[xf], 0.0)
-    nzs[...] = routed
+        routed = routed + jnp.where(nxb[xf, 1:2] == here, nxb[xf, 0:1], 0.0)
+    nzs[0] = routed
     nzb[mine] = routed
     for d in FAR_FIRST:
-        copy = remote(nzs, nzb.at[mine], nzsm.at[d], nzr.at[mine], dev(x, y, (z + d) % ZS, c))
+        copy = remote(nzs.at[0], nzb.at[mine], nzsm.at[d], nzr.at[mine], dev(x, y, (z + d) % ZS, c))
         copy.start()
         sends.append(copy)
+
+    for n in range(PARTS - 1):
+        part = slice(n * PART, (n + 1) * PART)
+        numb[mine] = numb[mine] + jnp.dot(phiq[n, mine], pbuf[mine, part], preferred_element_type=F32)
+        for d in FAR_FIRST:
+            i = head_of((z + ZS - d) % ZS)
+            remote(pbuf.at[i, part], pbuf.at[i, part], ps.at[n, d], pr.at[n, i], sibling).wait_recv()
+            numb[i] = numb[i] + jnp.dot(phiq[n, i], pbuf[i, part], preferred_element_type=F32)
 
     for d in range(1, 4):
         member = (me4 + d) % 4
@@ -307,50 +317,53 @@
     def _():
         for d in range(1, XS):
             xf = (x + d) % XS
-            remote(dsend, dbuf.at[xf], dsm.at[d], dr.at[xf], sibling).wait_recv()
-        state = jnp.zeros((4, 32, 256), F32)
+            remote(wholeb, dbuf.at[xf], dsm.at[d], dr.at[xf], sibling).wait_recv()
+        state = jnp.zeros((ROWS, LANES), F32)
         for xf in range(XS):
-            state = state + jnp.where(dbuf[xf, :, :, 255:256] == here, dbuf[xf], 0.0)
-        drt[...] = state
+            state = state + jnp.where(dbuf[xf, :, LANES - 1 :] == here, dbuf[xf], 0.0)
+        dt[...] = jnp.concatenate([state, jnp.zeros((256 - ROWS, LANES), F32)], 0).T
+        for sub in range(4):
+            drt[sub] = dt[28 * sub : 28 * sub + 32, :]
         for copy in e_copies:
             copy.start()
         dfin[...] = drt[me4]
 
-    def finish(i):
-        num = numb[i] + jnp.dot(phiq[i], pbuf[i], preferred_element_type=F32)
+    last = slice((PARTS - 1) * PART, ROWS)
+
+    def finish(k, i):
+        num = numb[i] + jnp.dot(phiq[PARTS - 1, i], pbuf[i, last], preferred_element_type=F32)
         den = num[:, HV : HV + 1] + (1.0 - live_col)
         numb[i] = num * (live_col / den)
-
-    finish(mine)
-    for d in FAR_FIRST:
-        zf = (z + ZS - d) % ZS
-        i = head_of(zf)
-        for n in range(PARTS):
-            part = slice(n * PART, (n + 1) * PART)
-            remote(pbuf.at[i, part], pbuf.at[i, part], ps.at[n, d], pr.at[n, i], sibling).wait_recv()
-        finish(i)
-
+        osend[i] = numb[i, pl.ds(theirs, TOK), :].astype(BF16)
+        copy = remote(osend.at[i], orecv.at[i], osm.at[k], orm.at[i], sibling)
+        copy.start()
+        sends.append(copy)
+
+    finish(0, mine)
     for d in FAR_FIRST:
         i = head_of((z + ZS - d) % ZS)
-        remote(nzs, nzb.at[i], nzsm.at[d], nzr.at[i], sibling).wait_recv()
-    nss[...] = jnp.concatenate([nzb[i, 0:1, :] for i in range(HALF)], 0)
+        remote(pbuf.at[i, last], pbuf.at[i, last], ps.at[PARTS - 1, d], pr.at[PARTS - 1, i], sibling).wait_recv()
+        finish(d, i)
+
+    for d in FAR_FIRST:
+        i = head_of((z + ZS - d) % ZS)
+        remote(nzs.at[0], nzb.at[i], nzsm.at[d], nzr.at[i], sibling).wait_recv()
+    nss[...] = jnp.concatenate([nzb[i] for i in range(HALF)], 0)
     nfull[c] = nss[...]
     to_sib_n = remote(nss, nfull.at[c], nps.at[0], npr.at[0], sibling)
     to_sib_n.start()
     sends.append(to_sib_n)
 
-    for j in range(7):
-        left = numb[j]
-        if j:
-            left = pltpu.roll(left, 128 - 16 * j, 1)
-        right = pltpu.roll(numb[j + 1], HV - 16 * j, 1)
-        obuf[:, 128 * j : 128 * j + 128] = jnp.where(lane < HV - 16 * j, left, right).astype(BF16)
-    other_half = pl.multiple_of(COLS * (1 - c), 128)
-    out_send = remote(obuf.at[pl.ds(theirs, TOK)], mixed.at[:, pl.ds(half, COLS)], osm.at[0], orm.at[0], sibling)
-    out_send.start()
-    sends.append(out_send)
-    out_own = pltpu.make_async_copy(obuf.at[pl.ds(ours, TOK)], mixed.at[:, pl.ds(half, COLS)], lsem.at[9])
-    out_own.start()
+    def side_by_side(get, at):
+        for j in range(7):
+            left = get(j)
+            if j:
+                left = pltpu.roll(left, 128 - 16 * j, 1)
+            right = pltpu.roll(get(j + 1), HV - 16 * j, 1)
+            tile = jnp.where(lane < HV - 16 * j, left, right).astype(BF16)
+            mixed[:, pl.ds(pl.multiple_of(at + 128 * j, 128), 128)] = tile
+
+    side_by_side(lambda i: numb[i, pl.ds(ours, TOK), :], half)
 
     loads[8].wait()
 
@@ -361,14 +374,14 @@
     full = jnp.dot(dfin[:, 0:ROWS], sel_v[...], precision=lax.Precision.HIGHEST, preferred_element_type=F32)
     dstate[...] = full[0:28, None, 0:EXPAND]
     to_sib_n.wait_recv()
-    norms = nfull[...].reshape(HEADS, 256)[:, 0:ROWS]
+    norms = nfull[...].reshape(HEADS, ROWS)
     full = jnp.dot(norms, sel_v[...], precision=lax.Precision.HIGHEST, preferred_element_type=F32)
     dnorm[...] = full[:, 0:EXPAND]
 
-    out_own.wait()
-    remote(
-        obuf.at[pl.ds(theirs, TOK)], mixed.at[:, pl.ds(other_half, COLS)], osm.at[0], orm.at[0], sibling
-    ).wait_recv()
+    for i in range(HALF):
+        remote(osend.at[i], orecv.at[i], osm.at[0], orm.at[i], sibling).wait_recv()
+    side_by_side(lambda i: orecv[i].astype(F32), pl.multiple_of(COLS * (1 - c), 128))
+
     for copy in sends:
         copy.wait_send()
 
@@ -386,7 +399,6 @@
 def on_device(tokens_in, query_weight, key_weight, value_weight, conv_weight, prompt_lengths, decode_map):
     sel = jnp.asarray(selection())
     hbm = pl.BlockSpec(memory_space=pltpu.HBM)
-    any_space = pl.BlockSpec(memory_space=pl.ANY)
     vmem = pl.BlockSpec(memory_space=pltpu.VMEM)
     smem = pl.BlockSpec(memory_space=pltpu.SMEM)
     dma = pltpu.SemaphoreType.DMA
@@ -398,7 +410,7 @@
             jax.ShapeDtypeStruct((HEADS, EXPAND), F32),
         ),
         in_specs=[hbm] * 5 + [smem] * 2 + [hbm],
-        out_specs=(any_space, vmem, vmem),
+        out_specs=(vmem, vmem, vmem),
         scratch_shapes=[
             pltpu.VMEM((CHIP + HALO, D), BF16),
             pltpu.VMEM((D, 256), BF16),
@@ -411,7 +423,7 @@
             pltpu.VMEM((HALF, CHIP, LANES), BF16),
             pltpu.VMEM((HALF, 32, CHIP), F32),
             pltpu.VMEM((HALF, ROWS, CHIP), BF16),
-            pltpu.VMEM((HALF, CHIP, ROWS), BF16),
+            pltpu.VMEM((PARTS, HALF, CHIP, PART), BF16),
             pltpu.VMEM((LANES, CHIP), BF16),
             pltpu.VMEM((HALF, CHIP, LANES), F32),
             pltpu.VMEM((HALF, ROWS, LANES), BF16),
@@ -420,19 +432,19 @@
             pltpu.VMEM((YS, ROWS, LANES), BF16),
             pltpu.VMEM((ZS, ROWS, LANES), BF16),
             pltpu.VMEM((HALF, ROWS, LANES), BF16),
-            pltpu.VMEM((256, LANES), F32),
+            pltpu.VMEM((ROWS, LANES), F32),
             pltpu.VMEM((LANES, 256), F32),
-            pltpu.VMEM((4, 32, 256), F32),
-            pltpu.VMEM((XS, 4, 32, 256), F32),
+            pltpu.VMEM((XS, ROWS, LANES), F32),
             pltpu.VMEM((4, 32, 256), F32),
             pltpu.VMEM((32, 256), F32),
-            pltpu.VMEM((8, 256), F32),
-            pltpu.VMEM((XS, 8, 256), F32),
-            pltpu.VMEM((8, 256), F32),
-            pltpu.VMEM((HALF, 8, 256), F32),
-            pltpu.VMEM((HALF, 256), F32),
-            pltpu.VMEM((2, HALF, 256), F32),
-            pltpu.VMEM((CHIP, COLS), BF16),
+            pltpu.VMEM((8, ROWS), F32),
+            pltpu.VMEM((XS, 8, ROWS), F32),
+            pltpu.VMEM((1, 1, ROWS), F32),
+            pltpu.VMEM((HALF, 1, ROWS), F32),
+            pltpu.VMEM((HALF, ROWS), F32),
+            pltpu.VMEM((2, HALF, ROWS), F32),
+            pltpu.VMEM((HALF, TOK, LANES), BF16),
+            pltpu.VMEM((HALF, TOK, LANES), BF16),
             dma((10,)),
             dma((3,)),
             dma((2,)),
@@ -452,8 +464,8 @@
             dma((ZS,)),
             dma((1,)),
             dma((1,)),
-            dma((1,)),
-            dma((1,)),
+            dma((8,)),
+            dma((8,)),
         ],
         compiler_params=pltpu.CompilerParams(
             collective_id=0, has_side_effects=True, vmem_limit_bytes=40 * 1024 * 1024

time: 44.2 us -> 45.4 us (1.027)
  Pallas kernels: 40.2 us -> 41.4 us
    pallas_call x1, Pallas kernels: 40.2 us -> 41.4 us  [on_device(): pl.pallas_call(kernel, out_shape=(jax.ShapeDtypeStruct((TOK, D), BF16), j...]
where the time goes in v3:
time: 45.4 us; the launch traced here: 45.3 us
  Pallas kernels  41.4 us (91%)
  local copies, waits for them, and re-layouts  1.99 us (4%)
  between operations  1.93 us (4%)
    pallas_call x1, Pallas kernels, on_device(): pl.pallas_call(kernel, out_shape=(jax.ShapeDtypeStruct((TOK, D), BF16), j...  41.4 us
    unnamed x3, local copies, waits for them, and re-layouts  1.99 us

profile of v3, /device:TPU:1, one launch (start us, length us, event | category | flops | bytes accessed | tf_op | source)
XLA Modules:
  0.0 45.3 jit_solution(9655781490940947666)
XLA Ops:
  1.9 41.4 %taylor_attention.1 = (bf16[128,1792]{1,0:T(8,128)(2,1)S(1)}, f32[28,1,273]{2,1,0:T(1,128)S(1)}, f32[16,273]{1,0:T(8,128)S(1)}) custom-call(bf16[128,1792]{1,0:T(8,128)(2,1)} %bitcast.9, bf16[1792,256]{1,0:T(8,128)(2,1)} %wq.1, bf16[1792,256]{1,0:T(8,128)(2,1)} %wk.1, bf16[1792,1792]{1,0:T(8,128)(2,1)} %wv.1, f32[3,1792]{1,0:T(4,128)} %cw.1, ...), custom_call_target="tpu_custom_call" | custom-call | flops 2000000000 | bytes 8000000 | tf_op jit(solution)/shard_map/taylor_attention/pallas_call | solution.py:405
  43.3 0.8 %copy.16 = bf16[1,128,1792]{2,1,0:T(8,128)(2,1)} copy(bf16[1,128,1792]{2,1,0:T(8,128)(2,1)S(1)} %bitcast.6) | data formatting | bytes 917504
  44.1 0.6 %copy.17 = f32[1,273,28]{1,0,2:T(1,128)} copy(f32[1,273,28]{1,0,2:T(1,128)S(1)} %bitcast.7) | data formatting | bytes 61152
  44.7 0.6 %copy.18 = f32[1,273,16]{1,2,0:T(8,128)} copy(f32[1,273,16]{1,2,0:T(8,128)S(1)} %bitcast.8) | data formatting | bytes 34944

commit v4 on v3

--- a/solution.py
+++ b/solution.py
@@ -70,8 +70,9 @@
     mixed, dstate, dnorm,
     xs, wqk_v, wv_v, cw_v, sel_v,
     qkb, vbuf, cvb, vp, yy, phik, phiq, ktb, numb, gsend, gat, tsend, ty, psend, pbuf,
-    wholeb, dt, dbuf, drt, dfin, nsend, nxb, nzs, nzb, nss, nfull, osend, orecv,
-    lsem, xsend, xrecv, gs, gr, ys, yr, ps, pr, dsm, dr, des, der, ns, nr, nzsm, nzr, nps, npr, osm, orm,
+    wholeb, dt, dbuf, drt, dfin, nys, nyb, nxs, nxb, nzs, nzr_b, nzo, nzb, nss, nfull, osend, orecv,
+    lsem, xsend, xrecv, gs, gr, ys, yr, ps, pr, dsm, dr, des, der,
+    nysm, nyr, nxsm, nxr, nzsm, nzr, nbs, nbr, nps, npr, osm, orm,
 ):
     x = lax.axis_index("req")
     blk = lax.axis_index("blk")
@@ -126,7 +127,11 @@
         pl.semaphore_signal(barrier, inc=1, device_id=device, device_id_type=MESH)
 
     here_i_am(sibling)
-    here_i_am((prv * 2 + 1, x))
+
+    @pl.when(chip > 0)
+    def _():
+        here_i_am((prv * 2 + 1, x))
+
     for d in FAR_FIRST:
         here_i_am(dev(x, y, (z + d) % ZS, c))
     for d in range(1, YS):
@@ -138,18 +143,26 @@
     def _():
         here_i_am(lead)
 
-    pl.semaphore_wait(barrier, 1 + (ZS - 1) + (YS - 1) + (XS - 1) + 2 * c + 3 * leads_int)
+    last_not = (chip < YS * ZS - 1).astype(jnp.int32)
+    pl.semaphore_wait(barrier, 1 + (ZS - 1) + (YS - 1) + (XS - 1) + 2 * c * last_not + 3 * leads_int)
 
     to_sib = remote(tok, xs.at[TOK:CHIP], xsend.at[0], xrecv.at[0], sibling)
-    to_sib.start()
     tail = tok.at[TOK - HALO : TOK]
     halo0 = remote(tail, xs.at[CHIP : CHIP + HALO], xsend.at[1], xrecv.at[1], (nxt * 2, x))
     halo1 = remote(tail, xs.at[CHIP : CHIP + HALO], xsend.at[2], xrecv.at[1], (nxt * 2 + 1, x))
 
-    @pl.when(c == 1)
+    sends_halo = (c == 1) & (chip < YS * ZS - 1)
+
+    @pl.when(sends_halo)
     def _():
         halo0.start()
         halo1.start()
+
+    to_sib.start()
+
+    @pl.when(chip == 0)
+    def _():
+        xs[CHIP:, :] = jnp.zeros((HALO, D), BF16)
 
     slot = dmap[0].astype(F32)
     length = plen[0]
@@ -172,7 +185,11 @@
         vbuf[pl.ds(v_ours, TOK), at : at + size] = val.astype(BF16).astype(F32)
     to_sib.wait_recv()
     qkb[pl.ds(theirs, TOK), :] = jnp.dot(xs[TOK:CHIP, :], wqk_v[...], preferred_element_type=F32)
-    halo1.wait_recv()
+
+    @pl.when(chip > 0)
+    def _():
+        halo1.wait_recv()
+
 
     keys_t = qkb[:, 0:128].T
     ktb[...] = keys_t.astype(BF16)
@@ -180,12 +197,11 @@
     phik[...] = phi.astype(BF16)
 
     loads[3].wait()
-    first = (chip > 0).astype(F32)
     for n, (at, size) in enumerate(VCHUNKS):
         val = jnp.dot(xs[TOK:, :], wv_v[:, at : at + size], preferred_element_type=F32)
         val = val.astype(BF16).astype(F32)
         vbuf[pl.ds(v_theirs, TOK), at : at + size] = val[0:TOK]
-        vbuf[0:HALO, at : at + size] = val[TOK:] * first
+        vbuf[0:HALO, at : at + size] = val[TOK:]
     for n, (at, size) in enumerate(VCHUNKS):
         conv = jnp.zeros((CHIP, size), F32)
         for tap in range(CONV):
@@ -212,6 +228,21 @@
             sends.append(copy)
         gat[z, part] = jnp.dot(phik[mine, part], vp[mine], preferred_element_type=F32).astype(BF16)
 
+    here = x.astype(F32)
+    wide = lax.broadcasted_iota(jnp.int32, (1, 256), 1)
+    row8 = lax.broadcasted_iota(jnp.int32, (HALF, 1), 0)
+    ones = jnp.ones((HALF, CHIP), BF16)
+    sums = jnp.zeros((HALF, ROWS), F32)
+    for i in range(HALF):
+        head_sum = lax.dot_general(ones, phik[i], (((1,), (1,)), ((), ())), preferred_element_type=F32)
+        sums = jnp.where(row8 == i, head_sum, sums)
+    nys[...] = sums
+    nyb[y] = sums
+    for d in (2, 1, 3):
+        copy = remote(nys, nyb.at[y], nysm.at[d], nyr.at[y], dev(x, (y + d) % YS, z, c))
+        copy.start()
+        sends.append(copy)
+
     queries = qkb[:, 128:256]
     phi_q = features((queries.T).reshape(HALF, FEAT, CHIP) * 0.5, yy, None)
     for i in range(HALF):
@@ -225,6 +256,17 @@
         dots = jnp.dot(one_head, ktb[...], preferred_element_type=F32) * 0.25
         weights = (1.0 + dots + 0.5 * dots * dots) * causal
         numb[i] = jnp.dot(weights.astype(BF16), vp[i], preferred_element_type=F32)
+
+    for d in range(1, YS):
+        yf = (y + d) % YS
+        remote(nys, nyb.at[yf], nysm.at[d], nyr.at[yf], sibling).wait_recv()
+    nxs[:, 0:ROWS] = nyb[0] + nyb[1] + nyb[2] + nyb[3]
+    nxs[:, ROWS:] = jnp.zeros((HALF, 256 - ROWS), F32) + slot
+    nxb[x] = nxs[...]
+    for d in (2, 1, 3):
+        copy = remote(nxs, nxb.at[x], nxsm.at[d], nxr.at[x], dev((x + d) % XS, y, z, c))
+        copy.start()
+        sends.append(copy)
 
     for n in range(PARTS):
         part = slice(n * PART, (n + 1) * PART)
@@ -243,6 +285,22 @@
             sends.append(copy)
         ty[y, part] = total.astype(BF16)
 
+    for d in range(1, XS):
+        xf = (x + d) % XS
+        remote(nxs, nxb.at[xf], nxsm.at[d], nxr.at[xf], sibling).wait_recv()
+    routed = jnp.zeros((HALF, 256), F32)
+    for xf in range(XS):
+        routed = routed + jnp.where(nxb[xf, :, 255:256] == here, nxb[xf], 0.0)
+    for i in range(HALF):
+        nzs[i] = routed[i : i + 1]
+    for d in FAR_FIRST:
+        zt = (z + d) % ZS
+        copy = remote(nzs.at[head_of(zt)], nzr_b.at[z], nzsm.at[d], nzr.at[z], dev(x, y, zt, c))
+        copy.start()
+        sends.append(copy)
+    nzr_b[z] = nzs[mine]
+
+    d_copies, e_copies = [], []
     for n in range(PARTS):
         part = slice(n * PART, (n + 1) * PART)
         for d in (2, 1, 3):
@@ -258,6 +316,18 @@
         for zz in range(ZS):
             psend[zz, part] = before.astype(BF16)
             before = before + gat[zz, part].astype(F32)
+        d_part = [
+            remote(wholeb.at[part], dbuf.at[x, part], dsm.at[n, d], dr.at[n, x], dev((x + d) % XS, y, z, c))
+            for d in (2, 1, 3)
+        ]
+
+        @pl.when(leads)
+        def _():
+            for copy in d_part:
+                copy.start()
+            dbuf[x, part] = wholeb[part]
+
+        d_copies += d_part
         for d in FAR_FIRST:
             zt = (z + d) % ZS
             copy = remote(psend.at[zt, part], pbuf.at[mine, part], ps.at[n, d], pr.at[n, mine], dev(x, y, zt, c))
@@ -265,37 +335,16 @@
             sends.append(copy)
         pbuf[mine, part] = psend[z, part]
 
-    here = x.astype(F32)
-    d_copies, e_copies = [], []
-    for d in (2, 1, 3):
-        d_copies.append(remote(wholeb, dbuf.at[x], dsm.at[d], dr.at[x], dev((x + d) % XS, y, z, c)))
-
-    @pl.when(leads)
-    def _():
-        for copy in d_copies:
-            copy.start()
-        dbuf[x] = wholeb[...]
-
-    row8 = lax.broadcasted_iota(jnp.int32, (8, LANES), 0)
-    pick = jnp.where((lane == HV) & (row8 == 0) | (lane == LANES - 1) & (row8 == 1), 1.0, 0.0)
-    nsend[...] = lax.dot_general(
-        pick, wholeb[...], (((1,), (1,)), ((), ())), precision=lax.Precision.HIGHEST, preferred_element_type=F32
-    )
-    nxb[x] = nsend[...]
-    for d in (2, 1, 3):
-        copy = remote(nsend, nxb.at[x], ns.at[d], nr.at[x], dev((x + d) % XS, y, z, c))
-        copy.start()
-        sends.append(copy)
-    for d in range(1, XS):
-        xf = (x + d) % XS
-        remote(nsend, nxb.at[xf], ns.at[d], nr.at[xf], sibling).wait_recv()
-    routed = jnp.zeros((1, ROWS), F32)
-    for xf in range(XS):
-        routed = routed + jnp.where(nxb[xf, 1:2] == here, nxb[xf, 0:1], 0.0)
-    nzs[0] = routed
-    nzb[mine] = routed
     for d in FAR_FIRST:
-        copy = remote(nzs.at[0], nzb.at[mine], nzsm.at[d], nzr.at[mine], dev(x, y, (z + d) % ZS, c))
+        zf = (z + ZS - d) % ZS
+        remote(nzs.at[0], nzr_b.at[zf], nzsm.at[d], nzr.at[zf], sibling).wait_recv()
+    whole_norm = nzr_b[0]
+    for zz in range(1, ZS):
+        whole_norm = whole_norm + nzr_b[zz]
+    nzo[0] = whole_norm
+    nzb[mine] = whole_norm
+    for d in FAR_FIRST:
+        copy = remote(nzo.at[0], nzb.at[mine], nbs.at[d], nbr.at[mine], dev(x, y, (z + d) % ZS, c))
         copy.start()
         sends.append(copy)
 
@@ -315,9 +364,11 @@
 
     @pl.when(leads)
     def _():
-        for d in range(1, XS):
-            xf = (x + d) % XS
-            remote(wholeb, dbuf.at[xf], dsm.at[d], dr.at[xf], sibling).wait_recv()
+        for n in range(PARTS):
+            part = slice(n * PART, (n + 1) * PART)
+            for d in range(1, XS):
+                xf = (x + d) % XS
+                remote(wholeb.at[part], dbuf.at[xf, part], dsm.at[n, d], dr.at[n, xf], sibling).wait_recv()
         state = jnp.zeros((ROWS, LANES), F32)
         for xf in range(XS):
             state = state + jnp.where(dbuf[xf, :, LANES - 1 :] == here, dbuf[xf], 0.0)
@@ -330,29 +381,26 @@
 
     last = slice((PARTS - 1) * PART, ROWS)
 
-    def finish(k, i):
+    for d in FAR_FIRST:
+        i = head_of((z + ZS - d) % ZS)
+        remote(nzo.at[0], nzb.at[i], nbs.at[d], nbr.at[i], sibling).wait_recv()
+    nss[...] = jnp.concatenate([nzb[i, :, 0:ROWS] for i in range(HALF)], 0)
+    nfull[c] = nss[...]
+    to_sib_n = remote(nss, nfull.at[c], nps.at[0], npr.at[0], sibling)
+    to_sib_n.start()
+    sends.append(to_sib_n)
+
+    for d in FAR_FIRST:
+        i = head_of((z + ZS - d) % ZS)
+        remote(pbuf.at[i, last], pbuf.at[i, last], ps.at[PARTS - 1, d], pr.at[PARTS - 1, i], sibling).wait_recv()
+    for i in range(HALF):
         num = numb[i] + jnp.dot(phiq[PARTS - 1, i], pbuf[i, last], preferred_element_type=F32)
         den = num[:, HV : HV + 1] + (1.0 - live_col)
         numb[i] = num * (live_col / den)
         osend[i] = numb[i, pl.ds(theirs, TOK), :].astype(BF16)
-        copy = remote(osend.at[i], orecv.at[i], osm.at[k], orm.at[i], sibling)
-        copy.start()
-        sends.append(copy)
-
-    finish(0, mine)
-    for d in FAR_FIRST:
-        i = head_of((z + ZS - d) % ZS)
-        remote(pbuf.at[i, last], pbuf.at[i, last], ps.at[PARTS - 1, d], pr.at[PARTS - 1, i], sibling).wait_recv()
-        finish(d, i)
-
-    for d in FAR_FIRST:
-        i = head_of((z + ZS - d) % ZS)
-        remote(nzs.at[0], nzb.at[i], nzsm.at[d], nzr.at[i], sibling).wait_recv()
-    nss[...] = jnp.concatenate([nzb[i] for i in range(HALF)], 0)
-    nfull[c] = nss[...]
-    to_sib_n = remote(nss, nfull.at[c], nps.at[0], npr.at[0], sibling)
-    to_sib_n.start()
-    sends.append(to_sib_n)
+    out_send = remote(osend, orecv, osm.at[0], orm.at[0], sibling)
+    out_send.start()
+    sends.append(out_send)
 
     def side_by_side(get, at):
         for j in range(7):
@@ -378,14 +426,13 @@
     full = jnp.dot(norms, sel_v[...], precision=lax.Precision.HIGHEST, preferred_element_type=F32)
     dnorm[...] = full[:, 0:EXPAND]
 
-    for i in range(HALF):
-        remote(osend.at[i], orecv.at[i], osm.at[0], orm.at[i], sibling).wait_recv()
+    out_send.wait_recv()
     side_by_side(lambda i: orecv[i].astype(F32), pl.multiple_of(COLS * (1 - c), 128))
 
     for copy in sends:
         copy.wait_send()
 
-    @pl.when(c == 1)
+    @pl.when(sends_halo)
     def _():
         halo0.wait_send()
         halo1.wait_send()
@@ -437,15 +484,19 @@
             pltpu.VMEM((XS, ROWS, LANES), F32),
             pltpu.VMEM((4, 32, 256), F32),
             pltpu.VMEM((32, 256), F32),
-            pltpu.VMEM((8, ROWS), F32),
-            pltpu.VMEM((XS, 8, ROWS), F32),
-            pltpu.VMEM((1, 1, ROWS), F32),
-            pltpu.VMEM((HALF, 1, ROWS), F32),
+            pltpu.VMEM((HALF, ROWS), F32),
+            pltpu.VMEM((YS, HALF, ROWS), F32),
+            pltpu.VMEM((HALF, 256), F32),
+            pltpu.VMEM((XS, HALF, 256), F32),
+            pltpu.VMEM((HALF, 1, 256), F32),
+            pltpu.VMEM((ZS, 1, 256), F32),
+            pltpu.VMEM((1, 1, 256), F32),
+            pltpu.VMEM((HALF, 1, 256), F32),
             pltpu.VMEM((HALF, ROWS), F32),
             pltpu.VMEM((2, HALF, ROWS), F32),
             pltpu.VMEM((HALF, TOK, LANES), BF16),
             pltpu.VMEM((HALF, TOK, LANES), BF16),
-            dma((10,)),
+            dma((9,)),
             dma((3,)),
             dma((2,)),
             dma((PARTS, ZS)),
@@ -454,18 +505,22 @@
             dma((PARTS, YS)),
             dma((PARTS, ZS)),
             dma((PARTS, ZS)),
-            dma((XS,)),
-            dma((XS,)),
+            dma((PARTS, XS)),
+            dma((PARTS, XS)),
             dma((4,)),
             dma((1,)),
+            dma((YS,)),
+            dma((YS,)),
             dma((XS,)),
             dma((XS,)),
             dma((ZS,)),
             dma((ZS,)),
+            dma((ZS,)),
+            dma((ZS,)),
             dma((1,)),
             dma((1,)),
-            dma((8,)),
-            dma((8,)),
+            dma((1,)),
+            dma((1,)),
         ],
         compiler_params=pltpu.CompilerParams(
             collective_id=0, has_side_effects=True, vmem_limit_bytes=40 * 1024 * 1024

time: 45.4 us -> 43.1 us (0.949)
  Pallas kernels: 41.4 us -> 39.1 us
    pallas_call x1, Pallas kernels: 41.4 us -> 39.1 us  [on_device(): pl.pallas_call(kernel, out_shape=(jax.ShapeDtypeStruct((TOK, D), BF16), j...]
where the time goes in v4:
time: 43.1 us; the launch traced here: 43 us
  Pallas kernels  39.1 us (91%)
  local copies, waits for them, and re-layouts  1.99 us (5%)
  between operations  1.93 us (4%)
    pallas_call x1, Pallas kernels, on_device(): pl.pallas_call(kernel, out_shape=(jax.ShapeDtypeStruct((TOK, D), BF16), j...  39.1 us
    unnamed x3, local copies, waits for them, and re-layouts  1.99 us

profile of v4, /device:TPU:1, one launch (start us, length us, event | category | flops | bytes accessed | tf_op | source)
XLA Modules:
  0.0 43.0 jit_solution(10394573592369773841)
XLA Ops:
  1.9 39.1 %taylor_attention.1 = (bf16[128,1792]{1,0:T(8,128)(2,1)S(1)}, f32[28,1,273]{2,1,0:T(1,128)S(1)}, f32[16,273]{1,0:T(8,128)S(1)}) custom-call(bf16[128,1792]{1,0:T(8,128)(2,1)} %bitcast.9, bf16[1792,256]{1,0:T(8,128)(2,1)} %wq.1, bf16[1792,256]{1,0:T(8,128)(2,1)} %wk.1, bf16[1792,1792]{1,0:T(8,128)(2,1)} %wv.1, f32[3,1792]{1,0:T(4,128)} %cw.1, ...), custom_call_target="tpu_custom_call" | custom-call | flops 2000000000 | bytes 8000000 | tf_op jit(solution)/shard_map/taylor_attention/pallas_call | solution.py:452
  41.0 0.8 %copy.16 = bf16[1,128,1792]{2,1,0:T(8,128)(2,1)} copy(bf16[1,128,1792]{2,1,0:T(8,128)(2,1)S(1)} %bitcast.6) | data formatting | bytes 917504
  41.8 0.6 %copy.17 = f32[1,273,28]{1,0,2:T(1,128)} copy(f32[1,273,28]{1,0,2:T(1,128)S(1)} %bitcast.7) | data formatting | bytes 61152
  42.4 0.6 %copy.18 = f32[1,273,16]{1,2,0:T(8,128)} copy(f32[1,273,16]{1,2,0:T(8,128)S(1)} %bitcast.8) | data formatting | bytes 34944

commit v5 on v4

--- a/solution.py
+++ b/solution.py
@@ -19,7 +19,7 @@
 COLS = HALF * HV
 TOK = 128
 CHIP = 2 * TOK
-HALO = 16
+HALO = 8
 ROWS = 160
 LANES = 128
 MESH = pl.DeviceIdType.MESH
@@ -186,15 +186,14 @@
     to_sib.wait_recv()
     qkb[pl.ds(theirs, TOK), :] = jnp.dot(xs[TOK:CHIP, :], wqk_v[...], preferred_element_type=F32)
 
-    @pl.when(chip > 0)
-    def _():
-        halo1.wait_recv()
-
-
     keys_t = qkb[:, 0:128].T
     ktb[...] = keys_t.astype(BF16)
     phi = features(keys_t.reshape(HALF, FEAT, CHIP) * 0.5, yy, live_row[None])
     phik[...] = phi.astype(BF16)
+
+    @pl.when(chip > 0)
+    def _():
+        halo1.wait_recv()
 
     loads[3].wait()
     for n, (at, size) in enumerate(VCHUNKS):

time: 43.1 us -> 42.1 us (0.977)
  Pallas kernels: 39.1 us -> 38 us
    pallas_call x1, Pallas kernels: 39.1 us -> 38 us  [on_device(): pl.pallas_call(kernel, out_shape=(jax.ShapeDtypeStruct((TOK, D), BF16), j...]
where the time goes in v5:
time: 42.1 us; the launch traced here: 42 us
  Pallas kernels  38 us (90%)
  local copies, waits for them, and re-layouts  1.99 us (5%)
  between operations  1.93 us (5%)
    pallas_call x1, Pallas kernels, on_device(): pl.pallas_call(kernel, out_shape=(jax.ShapeDtypeStruct((TOK, D), BF16), j...  38 us
    unnamed x3, local copies, waits for them, and re-layouts  1.99 us

profile of v5, /device:TPU:1, one launch (start us, length us, event | category | flops | bytes accessed | tf_op | source)
XLA Modules:
  0.0 42.0 jit_solution(1497994902915182420)
XLA Ops:
  1.9 38.0 %taylor_attention.1 = (bf16[128,1792]{1,0:T(8,128)(2,1)S(1)}, f32[28,1,273]{2,1,0:T(1,128)S(1)}, f32[16,273]{1,0:T(8,128)S(1)}) custom-call(bf16[128,1792]{1,0:T(8,128)(2,1)} %bitcast.9, bf16[1792,256]{1,0:T(8,128)(2,1)} %wq.1, bf16[1792,256]{1,0:T(8,128)(2,1)} %wk.1, bf16[1792,1792]{1,0:T(8,128)(2,1)} %wv.1, f32[3,1792]{1,0:T(4,128)} %cw.1, ...), custom_call_target="tpu_custom_call" | custom-call | flops 2000000000 | bytes 8000000 | tf_op jit(solution)/shard_map/taylor_attention/pallas_call | solution.py:451
  40.0 0.8 %copy.16 = bf16[1,128,1792]{2,1,0:T(8,128)(2,1)} copy(bf16[1,128,1792]{2,1,0:T(8,128)(2,1)S(1)} %bitcast.6) | data formatting | bytes 917504
  40.7 0.6 %copy.17 = f32[1,273,28]{1,0,2:T(1,128)} copy(f32[1,273,28]{1,0,2:T(1,128)S(1)} %bitcast.7) | data formatting | bytes 61152
  41.4 0.6 %copy.18 = f32[1,273,16]{1,2,0:T(8,128)} copy(f32[1,273,16]{1,2,0:T(8,128)S(1)} %bitcast.8) | data formatting | bytes 34944

commit v6 on v5

--- a/solution.py
+++ b/solution.py
@@ -218,14 +218,15 @@
     sends = [to_sib]
     for n in range(PARTS):
         part = slice(n * PART, (n + 1) * PART)
+        for i in range(HALF):
+            gsend[i, part] = jnp.dot(phik[i, part], vp[i], preferred_element_type=F32).astype(BF16)
         for d in FAR_FIRST:
             zt = (z + d) % ZS
             i = head_of(zt)
-            gsend[i, part] = jnp.dot(phik[i, part], vp[i], preferred_element_type=F32).astype(BF16)
             copy = remote(gsend.at[i, part], gat.at[z, part], gs.at[n, d], gr.at[n, z], dev(x, y, zt, c))
             copy.start()
             sends.append(copy)
-        gat[z, part] = jnp.dot(phik[mine, part], vp[mine], preferred_element_type=F32).astype(BF16)
+        gat[z, part] = gsend[mine, part]
 
     here = x.astype(F32)
     wide = lax.broadcasted_iota(jnp.int32, (1, 256), 1)

time: 42.1 us -> 41.7 us (level)
  no operation moved by 1% of the time
where the time goes in v6:
time: 41.7 us; the launch traced here: 41.6 us
  Pallas kernels  37.6 us (90%)
  local copies, waits for them, and re-layouts  1.99 us (5%)
  between operations  1.93 us (5%)
    pallas_call x1, Pallas kernels, on_device(): pl.pallas_call(kernel, out_shape=(jax.ShapeDtypeStruct((TOK, D), BF16), j...  37.6 us
    unnamed x3, local copies, waits for them, and re-layouts  1.99 us

profile of v6, /device:TPU:1, one launch (start us, length us, event | category | flops | bytes accessed | tf_op | source)
XLA Modules:
  0.0 41.6 jit_solution(2416784180969710391)
XLA Ops:
  1.9 37.6 %taylor_attention.1 = (bf16[128,1792]{1,0:T(8,128)(2,1)S(1)}, f32[28,1,273]{2,1,0:T(1,128)S(1)}, f32[16,273]{1,0:T(8,128)S(1)}) custom-call(bf16[128,1792]{1,0:T(8,128)(2,1)} %bitcast.9, bf16[1792,256]{1,0:T(8,128)(2,1)} %wq.1, bf16[1792,256]{1,0:T(8,128)(2,1)} %wk.1, bf16[1792,1792]{1,0:T(8,128)(2,1)} %wv.1, f32[3,1792]{1,0:T(4,128)} %cw.1, ...), custom_call_target="tpu_custom_call" | custom-call | flops 2000000000 | bytes 8000000 | tf_op jit(solution)/shard_map/taylor_attention/pallas_call | solution.py:452
  39.6 0.8 %copy.16 = bf16[1,128,1792]{2,1,0:T(8,128)(2,1)} copy(bf16[1,128,1792]{2,1,0:T(8,128)(2,1)S(1)} %bitcast.6) | data formatting | bytes 917504
  40.3 0.6 %copy.17 = f32[1,273,28]{1,0,2:T(1,128)} copy(f32[1,273,28]{1,0,2:T(1,128)S(1)} %bitcast.7) | data formatting | bytes 61152
  41.0 0.6 %copy.18 = f32[1,273,16]{1,2,0:T(8,128)} copy(f32[1,273,16]{1,2,0:T(8,128)S(1)} %bitcast.8) | data formatting | bytes 34944

commit v7 on v6

--- a/solution.py
+++ b/solution.py
@@ -26,39 +26,42 @@
 VCHUNKS = ((0, 256), (256, 256), (512, 256), (768, 128))
 FAR_FIRST = (4, 3, 5, 2, 6, 1, 7)
 PARTS = 2
-PART = ROWS // PARTS
+TILE = 144
+PART_ROWS = (slice(0, 80), slice(80, TILE))
+PART_SIZE = (80, TILE - 80)
 F32 = jnp.float32
 BF16 = jnp.bfloat16
 
 
 def selection():
     sel = np.zeros((384, ROWS), np.float32)
-    sel[0, 152] = 1.0
+    sel[0, 136] = 1.0
     for a in range(16):
-        sel[1 + a, a] = 1.0
+        sel[1 + a, 144 + a if a < 15 else 137] = 1.0
         for b in range(16):
             row = 17 + 16 * a + b
             r = (b - a) % 16
             if r == 0:
-                sel[row, 16 + a] = 1.0
+                sel[row, a] = 1.0
             elif r < 8:
-                sel[row, 16 + 16 * r + a] = math.sqrt(0.5)
+                sel[row, 16 * r + a] = math.sqrt(0.5)
             elif r > 8:
-                sel[row, 16 + 16 * (16 - r) + b] = math.sqrt(0.5)
+                sel[row, 16 * (16 - r) + b] = math.sqrt(0.5)
             else:
-                sel[row, 144 + min(a, b)] = math.sqrt(0.5)
+                sel[row, 128 + min(a, b)] = math.sqrt(0.5)
     return sel.T.copy()
 
 
 def features(heads_t, yy, extra):
     yy[:, 0:16, :] = heads_t
     yy[:, 16:32, :] = heads_t
-    parts = [heads_t, heads_t * heads_t * math.sqrt(0.5)]
+    parts = [heads_t * heads_t * math.sqrt(0.5)]
     for r in range(1, 8):
         parts.append(heads_t * yy[:, r : r + 16, :])
     parts.append(heads_t[:, 0:8] * heads_t[:, 8:16])
     row = lax.broadcasted_iota(jnp.int32, (HALF, 8, CHIP), 1)
-    parts.append(jnp.where(row == 0, 1.0, 0.0).astype(F32))
+    parts.append(jnp.where(row == 0, 1.0, jnp.where(row == 1, heads_t[:, 15:16], 0.0)).astype(F32))
+    parts.append(heads_t)
     phi = jnp.concatenate(parts, 1)
     if extra is not None:
         phi = phi * extra
@@ -69,7 +72,7 @@
     tok, wq, wk, wv, cw, plen, dmap, sel,
     mixed, dstate, dnorm,
     xs, wqk_v, wv_v, cw_v, sel_v,
-    qkb, vbuf, cvb, vp, yy, phik, phiq, ktb, numb, gsend, gat, tsend, ty, psend, pbuf,
+    qkb, vbuf, cvb, vp, yy, phik, phiq, yqs, ktb, numb, stb, gsend, gat, tsend, ty, psend, pbuf,
     wholeb, dt, dbuf, drt, dfin, nys, nyb, nxs, nxb, nzs, nzr_b, nzo, nzb, nss, nfull, osend, orecv,
     lsem, xsend, xrecv, gs, gr, ys, yr, ps, pr, dsm, dr, des, der,
     nysm, nyr, nxsm, nxr, nzsm, nzr, nbs, nbr, nps, npr, osm, orm,
@@ -216,10 +219,18 @@
         vp[i] = head.astype(BF16)
 
     sends = [to_sib]
+    linear = []
+    for i in range(HALF):
+        state = jnp.dot(phik[i], vp[i], preferred_element_type=F32)
+        stb[i] = state[0:TILE]
+        linear.append(state[TILE:])
+    linear_t = jnp.concatenate(linear, 0).T
+    for i in range(HALF):
+        moved = pltpu.roll(linear_t, (HV + 1 - FEAT * i) % LANES, 1)
+        gsend[i, 0:LANES] = jnp.where(lane > HV, moved, stb[i, 0:LANES]).astype(BF16)
+        gsend[i, LANES:] = stb[i, LANES:].astype(BF16)
     for n in range(PARTS):
-        part = slice(n * PART, (n + 1) * PART)
-        for i in range(HALF):
-            gsend[i, part] = jnp.dot(phik[i, part], vp[i], preferred_element_type=F32).astype(BF16)
+        part = PART_ROWS[n]
         for d in FAR_FIRST:
             zt = (z + d) % ZS
             i = head_of(zt)
@@ -247,7 +258,9 @@
     phi_q = features((queries.T).reshape(HALF, FEAT, CHIP) * 0.5, yy, None)
     for i in range(HALF):
         for n in range(PARTS):
-            phiq[n, i] = phi_q[i, n * PART : (n + 1) * PART].T.astype(BF16)
+            phiq[n, i, :, 0 : PART_SIZE[n]] = phi_q[i, PART_ROWS[n]].T.astype(BF16)
+        spread = pltpu.roll(queries, (HV + 1 - FEAT * i) % LANES, 1)
+        yqs[i] = jnp.where(lane > HV, spread * 0.5, 0.0).astype(BF16)
     row_t = lax.broadcasted_iota(jnp.int32, (CHIP, CHIP), 0)
     col_s = lax.broadcasted_iota(jnp.int32, (CHIP, CHIP), 1)
     causal = jnp.where(row_t >= col_s, 1.0, 0.0).astype(F32) * live_row
@@ -269,7 +282,7 @@
         sends.append(copy)
 
     for n in range(PARTS):
-        part = slice(n * PART, (n + 1) * PART)
+        part = PART_ROWS[n]
         for d in FAR_FIRST:
             zf = (z + ZS - d) % ZS
             remote(gat.at[zf, part], gat.at[zf, part], gs.at[n, d], gr.at[n, zf], sibling).wait_recv()
@@ -302,17 +315,18 @@
 
     d_copies, e_copies = [], []
     for n in range(PARTS):
-        part = slice(n * PART, (n + 1) * PART)
+        part = PART_ROWS[n]
         for d in (2, 1, 3):
             yf = (y + YS - d) % YS
             remote(tsend.at[part], ty.at[yf, part], ys.at[n, d], yr.at[n, yf], sibling).wait_recv()
-        before = jnp.zeros((PART, LANES), F32)
-        whole = jnp.zeros((PART, LANES), F32)
+        before = jnp.zeros((PART_SIZE[n], LANES), F32)
+        whole = jnp.zeros((PART_SIZE[n], LANES), F32)
+        row_at = lax.broadcasted_iota(jnp.int32, (PART_SIZE[n], 1), 0) + part.start
         for yf in range(YS):
             piece = ty[yf, part].astype(F32)
             whole = whole + piece
             before = before + piece * (yf < y).astype(F32)
-        wholeb[part] = jnp.where(lane == LANES - 1, slot, whole)
+        wholeb[part] = jnp.where(row_at == TILE - 1, slot, whole)
         for zz in range(ZS):
             psend[zz, part] = before.astype(BF16)
             before = before + gat[zz, part].astype(F32)
@@ -349,12 +363,13 @@
         sends.append(copy)
 
     for n in range(PARTS - 1):
-        part = slice(n * PART, (n + 1) * PART)
-        numb[mine] = numb[mine] + jnp.dot(phiq[n, mine], pbuf[mine, part], preferred_element_type=F32)
+        part = PART_ROWS[n]
+        size = PART_SIZE[n]
+        numb[mine] = numb[mine] + jnp.dot(phiq[n, mine, :, 0:size], pbuf[mine, part], preferred_element_type=F32)
         for d in FAR_FIRST:
             i = head_of((z + ZS - d) % ZS)
             remote(pbuf.at[i, part], pbuf.at[i, part], ps.at[n, d], pr.at[n, i], sibling).wait_recv()
-            numb[i] = numb[i] + jnp.dot(phiq[n, i], pbuf[i, part], preferred_element_type=F32)
+            numb[i] = numb[i] + jnp.dot(phiq[n, i, :, 0:size], pbuf[i, part], preferred_element_type=F32)
 
     for d in range(1, 4):
         member = (me4 + d) % 4
@@ -365,21 +380,25 @@
     @pl.when(leads)
     def _():
         for n in range(PARTS):
-            part = slice(n * PART, (n + 1) * PART)
+            part = PART_ROWS[n]
             for d in range(1, XS):
                 xf = (x + d) % XS
                 remote(wholeb.at[part], dbuf.at[xf, part], dsm.at[n, d], dr.at[n, xf], sibling).wait_recv()
-        state = jnp.zeros((ROWS, LANES), F32)
+        state = jnp.zeros((TILE, LANES), F32)
         for xf in range(XS):
-            state = state + jnp.where(dbuf[xf, :, LANES - 1 :] == here, dbuf[xf], 0.0)
-        dt[...] = jnp.concatenate([state, jnp.zeros((256 - ROWS, LANES), F32)], 0).T
+            state = state + jnp.where(dbuf[xf, TILE - 1 :, :] == here, dbuf[xf], 0.0)
+        turned = jnp.concatenate([state, jnp.zeros((256 - TILE, LANES), F32)], 0).T
+        moved = pltpu.roll(state[0:LANES], 256 - LANES + TILE - LANES - HV - 1, 1)
+        dt[:, 0:LANES] = turned[:, 0:LANES]
+        spare = (lane >= TILE - LANES) & (lane < TILE - LANES + FEAT - 1)
+        dt[:, LANES:] = jnp.where(spare, moved, turned[:, LANES:])
         for sub in range(4):
             drt[sub] = dt[28 * sub : 28 * sub + 32, :]
         for copy in e_copies:
             copy.start()
         dfin[...] = drt[me4]
 
-    last = slice((PARTS - 1) * PART, ROWS)
+    last = PART_ROWS[PARTS - 1]
 
     for d in FAR_FIRST:
         i = head_of((z + ZS - d) % ZS)
@@ -394,7 +413,10 @@
         i = head_of((z + ZS - d) % ZS)
         remote(pbuf.at[i, last], pbuf.at[i, last], ps.at[PARTS - 1, d], pr.at[PARTS - 1, i], sibling).wait_recv()
     for i in range(HALF):
-        num = numb[i] + jnp.dot(phiq[PARTS - 1, i], pbuf[i, last], preferred_element_type=F32)
+        num = numb[i] + jnp.dot(phiq[PARTS - 1, i, :, 0 : PART_SIZE[-1]], pbuf[i, last], preferred_element_type=F32)
+        num = num + lax.dot_general(
+            yqs[i], pbuf[i, 0:LANES], (((1,), (1,)), ((), ())), preferred_element_type=F32
+        )
         den = num[:, HV : HV + 1] + (1.0 - live_col)
         numb[i] = num * (live_col / den)
         osend[i] = numb[i, pl.ds(theirs, TOK), :].astype(BF16)
@@ -470,18 +492,20 @@
             pltpu.VMEM((HALF, CHIP, LANES), BF16),
             pltpu.VMEM((HALF, 32, CHIP), F32),
             pltpu.VMEM((HALF, ROWS, CHIP), BF16),
-            pltpu.VMEM((PARTS, HALF, CHIP, PART), BF16),
+            pltpu.VMEM((PARTS, HALF, CHIP, PART_SIZE[0]), BF16),
+            pltpu.VMEM((HALF, CHIP, LANES), BF16),
             pltpu.VMEM((LANES, CHIP), BF16),
             pltpu.VMEM((HALF, CHIP, LANES), F32),
-            pltpu.VMEM((HALF, ROWS, LANES), BF16),
-            pltpu.VMEM((ZS, ROWS, LANES), BF16),
-            pltpu.VMEM((ROWS, LANES), BF16),
-            pltpu.VMEM((YS, ROWS, LANES), BF16),
-            pltpu.VMEM((ZS, ROWS, LANES), BF16),
-            pltpu.VMEM((HALF, ROWS, LANES), BF16),
-            pltpu.VMEM((ROWS, LANES), F32),
+            pltpu.VMEM((HALF, TILE, LANES), F32),
+            pltpu.VMEM((HALF, TILE, LANES), BF16),
+            pltpu.VMEM((ZS, TILE, LANES), BF16),
+            pltpu.VMEM((TILE, LANES), BF16),
+            pltpu.VMEM((YS, TILE, LANES), BF16),
+            pltpu.VMEM((ZS, TILE, LANES), BF16),
+            pltpu.VMEM((HALF, TILE, LANES), BF16),
+            pltpu.VMEM((TILE, LANES), F32),
             pltpu.VMEM((LANES, 256), F32),
-            pltpu.VMEM((XS, ROWS, LANES), F32),
+            pltpu.VMEM((XS, TILE, LANES), F32),
             pltpu.VMEM((4, 32, 256), F32),
             pltpu.VMEM((32, 256), F32),
             pltpu.VMEM((HALF, ROWS), F32),

time: 41.7 us -> 41 us (0.983)
  Pallas kernels: 37.6 us -> 36.9 us
    pallas_call x1, Pallas kernels: 37.6 us -> 36.9 us  [on_device(): pl.pallas_call(kernel, out_shape=(jax.ShapeDtypeStruct((TOK, D), BF16), j...]
where the time goes in v7:
time: 41 us; the launch traced here: 40.9 us
  Pallas kernels  36.9 us (90%)
  local copies, waits for them, and re-layouts  1.99 us (5%)
  between operations  1.93 us (5%)
    pallas_call x1, Pallas kernels, on_device(): pl.pallas_call(kernel, out_shape=(jax.ShapeDtypeStruct((TOK, D), BF16), j...  36.9 us
    unnamed x3, local copies, waits for them, and re-layouts  1.99 us

profile of v7, /device:TPU:1, one launch (start us, length us, event | category | flops | bytes accessed | tf_op | source)
XLA Modules:
  0.0 40.9 jit_solution(18422722089998975438)
XLA Ops:
  1.9 36.9 %taylor_attention.1 = (bf16[128,1792]{1,0:T(8,128)(2,1)S(1)}, f32[28,1,273]{2,1,0:T(1,128)S(1)}, f32[16,273]{1,0:T(8,128)S(1)}) custom-call(bf16[128,1792]{1,0:T(8,128)(2,1)} %bitcast.9, bf16[1792,256]{1,0:T(8,128)(2,1)} %wq.1, bf16[1792,256]{1,0:T(8,128)(2,1)} %wk.1, bf16[1792,1792]{1,0:T(8,128)(2,1)} %wv.1, f32[3,1792]{1,0:T(4,128)} %cw.1, ...), custom_call_target="tpu_custom_call" | custom-call | flops 2000000000 | bytes 8000000 | tf_op jit(solution)/shard_map/taylor_attention/pallas_call | solution.py:474
  38.9 0.8 %copy.16 = bf16[1,128,1792]{2,1,0:T(8,128)(2,1)} copy(bf16[1,128,1792]{2,1,0:T(8,128)(2,1)S(1)} %bitcast.6) | data formatting | bytes 917504
  39.6 0.6 %copy.17 = f32[1,273,28]{1,0,2:T(1,128)} copy(f32[1,273,28]{1,0,2:T(1,128)S(1)} %bitcast.7) | data formatting | bytes 61152
  40.3 0.6 %copy.18 = f32[1,273,16]{1,2,0:T(8,128)} copy(f32[1,273,16]{1,2,0:T(8,128)S(1)} %bitcast.8) | data formatting | bytes 34944

commit v8 on v7

--- a/solution.py
+++ b/solution.py
@@ -171,8 +171,6 @@
     length = plen[0]
     lane_tok = lax.broadcasted_iota(jnp.int32, (1, CHIP), 1) + chip * CHIP
     live_row = jnp.where(lane_tok < length, 1.0, 0.0).astype(F32)
-    sub_tok = lax.broadcasted_iota(jnp.int32, (CHIP, 1), 0) + chip * CHIP
-    live_col = jnp.where(sub_tok < length, 1.0, 0.0).astype(F32)
     lane = lax.broadcasted_iota(jnp.int32, (1, LANES), 1)
 
     ours = pl.multiple_of(TOK * c, TOK)
@@ -362,15 +360,6 @@
         copy.start()
         sends.append(copy)
 
-    for n in range(PARTS - 1):
-        part = PART_ROWS[n]
-        size = PART_SIZE[n]
-        numb[mine] = numb[mine] + jnp.dot(phiq[n, mine, :, 0:size], pbuf[mine, part], preferred_element_type=F32)
-        for d in FAR_FIRST:
-            i = head_of((z + ZS - d) % ZS)
-            remote(pbuf.at[i, part], pbuf.at[i, part], ps.at[n, d], pr.at[n, i], sibling).wait_recv()
-            numb[i] = numb[i] + jnp.dot(phiq[n, i, :, 0:size], pbuf[i, part], preferred_element_type=F32)
-
     for d in range(1, 4):
         member = (me4 + d) % 4
         e_copies.append(
@@ -398,6 +387,15 @@
             copy.start()
         dfin[...] = drt[me4]
 
+    for n in range(PARTS - 1):
+        part = PART_ROWS[n]
+        size = PART_SIZE[n]
+        numb[mine] = numb[mine] + jnp.dot(phiq[n, mine, :, 0:size], pbuf[mine, part], preferred_element_type=F32)
+        for d in FAR_FIRST:
+            i = head_of((z + ZS - d) % ZS)
+            remote(pbuf.at[i, part], pbuf.at[i, part], ps.at[n, d], pr.at[n, i], sibling).wait_recv()
+            numb[i] = numb[i] + jnp.dot(phiq[n, i, :, 0:size], pbuf[i, part], preferred_element_type=F32)
+
     last = PART_ROWS[PARTS - 1]
 
     for d in FAR_FIRST:
@@ -412,17 +410,26 @@
     for d in FAR_FIRST:
         i = head_of((z + ZS - d) % ZS)
         remote(pbuf.at[i, last], pbuf.at[i, last], ps.at[PARTS - 1, d], pr.at[PARTS - 1, i], sibling).wait_recv()
-    for i in range(HALF):
-        num = numb[i] + jnp.dot(phiq[PARTS - 1, i, :, 0 : PART_SIZE[-1]], pbuf[i, last], preferred_element_type=F32)
+    def finish(i, start):
+        rows = pl.ds(start, TOK)
+        at = lax.broadcasted_iota(jnp.int32, (TOK, 1), 0) + chip * CHIP + start
+        alive = jnp.where(at < length, 1.0, 0.0).astype(F32)
+        num = numb[i, rows, :] + jnp.dot(
+            phiq[PARTS - 1, i, rows, 0 : PART_SIZE[-1]], pbuf[i, last], preferred_element_type=F32
+        )
         num = num + lax.dot_general(
-            yqs[i], pbuf[i, 0:LANES], (((1,), (1,)), ((), ())), preferred_element_type=F32
+            yqs[i, rows, :], pbuf[i, 0:LANES], (((1,), (1,)), ((), ())), preferred_element_type=F32
         )
-        den = num[:, HV : HV + 1] + (1.0 - live_col)
-        numb[i] = num * (live_col / den)
-        osend[i] = numb[i, pl.ds(theirs, TOK), :].astype(BF16)
+        den = num[:, HV : HV + 1] + (1.0 - alive)
+        return num * (alive / den)
+
+    for i in range(HALF):
+        osend[i] = finish(i, theirs).astype(BF16)
     out_send = remote(osend, orecv, osm.at[0], orm.at[0], sibling)
     out_send.start()
     sends.append(out_send)
+    for i in range(HALF):
+        numb[i, pl.ds(ours, TOK), :] = finish(i, ours)
 
     def side_by_side(get, at):
         for j in range(7):

time: 41 us -> 40.9 us (level)
  no operation moved by 1% of the time
where the time goes in v8:
time: 40.9 us; the launch traced here: 40.8 us
  Pallas kernels  36.9 us (90%)
  local copies, waits for them, and re-layouts  1.99 us (5%)
  between operations  1.93 us (5%)
    pallas_call x1, Pallas kernels, on_device(): pl.pallas_call(kernel, out_shape=(jax.ShapeDtypeStruct((TOK, D), BF16), j...  36.9 us
    unnamed x3, local copies, waits for them, and re-layouts  1.99 us

profile of v8, /device:TPU:1, one launch (start us, length us, event | category | flops | bytes accessed | tf_op | source)
XLA Modules:
  0.0 40.8 jit_solution(5265742973242275681)
XLA Ops:
  1.9 36.9 %taylor_attention.1 = (bf16[128,1792]{1,0:T(8,128)(2,1)S(1)}, f32[28,1,273]{2,1,0:T(1,128)S(1)}, f32[16,273]{1,0:T(8,128)S(1)}) custom-call(bf16[128,1792]{1,0:T(8,128)(2,1)} %bitcast.9, bf16[1792,256]{1,0:T(8,128)(2,1)} %wq.1, bf16[1792,256]{1,0:T(8,128)(2,1)} %wk.1, bf16[1792,1792]{1,0:T(8,128)(2,1)} %wv.1, f32[3,1792]{1,0:T(4,128)} %cw.1, ...), custom_call_target="tpu_custom_call" | custom-call | flops 2000000000 | bytes 8000000 | tf_op jit(solution)/shard_map/taylor_attention/pallas_call | solution.py:481
  38.8 0.8 %copy.16 = bf16[1,128,1792]{2,1,0:T(8,128)(2,1)} copy(bf16[1,128,1792]{2,1,0:T(8,128)(2,1)S(1)} %bitcast.6) | data formatting | bytes 917504
  39.6 0.6 %copy.17 = f32[1,273,28]{1,0,2:T(1,128)} copy(f32[1,273,28]{1,0,2:T(1,128)S(1)} %bitcast.7) | data formatting | bytes 61152
  40.2 0.6 %copy.18 = f32[1,273,16]{1,2,0:T(8,128)} copy(f32[1,273,16]{1,2,0:T(8,128)S(1)} %bitcast.8) | data formatting | bytes 34944

commit v9 on v8

--- a/solution.py
+++ b/solution.py
@@ -27,8 +27,8 @@
 FAR_FIRST = (4, 3, 5, 2, 6, 1, 7)
 PARTS = 2
 TILE = 144
-PART_ROWS = (slice(0, 80), slice(80, TILE))
-PART_SIZE = (80, TILE - 80)
+PART_ROWS = (slice(0, 64), slice(64, TILE))
+PART_SIZE = (64, TILE - 64)
 F32 = jnp.float32
 BF16 = jnp.bfloat16
 
@@ -443,18 +443,17 @@
     side_by_side(lambda i: numb[i, pl.ds(ours, TOK), :], half)
 
     loads[8].wait()
-
-    @pl.when(jnp.logical_not(leads))
-    def _():
-        remote(dfin, dfin, des.at[0], der.at[0], sibling).wait_recv()
-
-    full = jnp.dot(dfin[:, 0:ROWS], sel_v[...], precision=lax.Precision.HIGHEST, preferred_element_type=F32)
-    dstate[...] = full[0:28, None, 0:EXPAND]
     to_sib_n.wait_recv()
     norms = nfull[...].reshape(HEADS, ROWS)
     full = jnp.dot(norms, sel_v[...], precision=lax.Precision.HIGHEST, preferred_element_type=F32)
     dnorm[...] = full[:, 0:EXPAND]
 
+    @pl.when(jnp.logical_not(leads))
+    def _():
+        remote(dfin, dfin, des.at[0], der.at[0], sibling).wait_recv()
+
+    full = jnp.dot(dfin[:, 0:ROWS], sel_v[...], precision=lax.Precision.HIGHEST, preferred_element_type=F32)
+    dstate[...] = full[0:28, None, 0:EXPAND]
     out_send.wait_recv()
     side_by_side(lambda i: orecv[i].astype(F32), pl.multiple_of(COLS * (1 - c), 128))
 
@@ -499,7 +498,7 @@
             pltpu.VMEM((HALF, CHIP, LANES), BF16),
             pltpu.VMEM((HALF, 32, CHIP), F32),
             pltpu.VMEM((HALF, ROWS, CHIP), BF16),
-            pltpu.VMEM((PARTS, HALF, CHIP, PART_SIZE[0]), BF16),
+            pltpu.VMEM((PARTS, HALF, CHIP, PART_SIZE[1]), BF16),
             pltpu.VMEM((HALF, CHIP, LANES), BF16),
             pltpu.VMEM((LANES, CHIP), BF16),
             pltpu.VMEM((HALF, CHIP, LANES), F32),

time: 40.9 us -> 40.7 us (level)
  no operation moved by 1% of the time
where the time goes in v9:
time: 40.7 us; the launch traced here: 40.6 us
  Pallas kernels  36.6 us (90%)
  local copies, waits for them, and re-layouts  1.99 us (5%)
  between operations  1.93 us (5%)
    pallas_call x1, Pallas kernels, on_device(): pl.pallas_call(kernel, out_shape=(jax.ShapeDtypeStruct((TOK, D), BF16), j...  36.6 us
    unnamed x3, local copies, waits for them, and re-layouts  1.99 us

profile of v9, /device:TPU:1, one launch (start us, length us, event | category | flops | bytes accessed | tf_op | source)
XLA Modules:
  0.0 40.6 jit_solution(627806710838417322)
XLA Ops:
  1.9 36.6 %taylor_attention.1 = (bf16[128,1792]{1,0:T(8,128)(2,1)S(1)}, f32[28,1,273]{2,1,0:T(1,128)S(1)}, f32[16,273]{1,0:T(8,128)S(1)}) custom-call(bf16[128,1792]{1,0:T(8,128)(2,1)} %bitcast.9, bf16[1792,256]{1,0:T(8,128)(2,1)} %wq.1, bf16[1792,256]{1,0:T(8,128)(2,1)} %wk.1, bf16[1792,1792]{1,0:T(8,128)(2,1)} %wv.1, f32[3,1792]{1,0:T(4,128)} %cw.1, ...), custom_call_target="tpu_custom_call" | custom-call | flops 2000000000 | bytes 8000000 | tf_op jit(solution)/shard_map/taylor_attention/pallas_call | solution.py:480
  38.6 0.8 %copy.16 = bf16[1,128,1792]{2,1,0:T(8,128)(2,1)} copy(bf16[1,128,1792]{2,1,0:T(8,128)(2,1)S(1)} %bitcast.6) | data formatting | bytes 917504
  39.3 0.6 %copy.17 = f32[1,273,28]{1,0,2:T(1,128)} copy(f32[1,273,28]{1,0,2:T(1,128)S(1)} %bitcast.7) | data formatting | bytes 61152
  40.0 0.6 %copy.18 = f32[1,273,16]{1,2,0:T(8,128)} copy(f32[1,273,16]{1,2,0:T(8,128)S(1)} %bitcast.8) | data formatting | bytes 34944
